TPU v7x, 32 devices: a whole 2x2x4 slice. The times are simulated.
32 devices in a mesh: row: 8 (over z, core), col: 4 (over y, x).
Axes of the slice: x: 2, y: 2, z: 4, core: 2. Of those that a mesh axis runs over, the one named last changes fastest.
Arguments:
- patches: bfloat16 [8, 4, 2, 16, 128, 128], P('row', 'col'), as said below
- windows: bfloat16 [8, 4, 2, 16, 36864], P('row', 'col'), as said below
- candidates: int32 [8, 4, 2, 2, 128], P('row', 'col'), may hold values from -32 to 32, as said below
- live: int32 [8, 4, 2], replicated, may hold values from 1 to 16, as said below
- edges: int32 [8, 2, 2820], P('row', None, 'col'), may hold values from 0 to 255, as said below
- stiffness: float32 [8, 2820], P('row', 'col'), may hold values from 0.3 to 3
Outputs:
- matches: float32 [8, 4, 2, 3, 16], P('row', 'col')
- mesh_shift: float32 [8, 4, 2, 256], P('row', 'col')
Inputs may be any that keep to these rules, and one draw needn't show every extreme that they name: `candidates`: the candidate shifts of a patch need not be distinct. live[r, c, k] counts the live slots of seam k of tile (r, c): slots 0 to live - 1; the same for all devices. Each tile's springs are the edges of its 16 x 16 vertex grid, horizontal and vertical, and one diagonal of every cell, in any order. `windows`: window k of tile (r, c) serves the seam that tile (r, c-1) (k = 0) or tile (r-1, c) (k = 1) holds as its seam k. `patches`: patch p of seam k is scored against window p of the neighbour.
All inputs are finite; a program needn't handle non-finite values.
Results may differ from a plain program's by a relative error of at most 0.0003.
Values may be sent and summed in bfloat16 or wider, within the bound.
A program may use at most 64 MiB of HBM per device.

v0:
```python
import jax
import jax.numpy as jnp
from jax import lax
from jax.sharding import PartitionSpec as P

REACH = 32
WIN = 192
NS = 8
P_SIZE = 16
BLK = 4
GV = 16
ITERS = 3


LAMBDA_REG = 0.05
EPSILON = 1e-05
PRECISE = lax.Precision.HIGHEST


def shifted(x, axis, by):
    length = lax.axis_size(axis)
    pairs = [(i, i + by) for i in range(length) if 0 <= i + by < length]
    return lax.ppermute(x, axis, pairs)


def with_halo(block, sides, width):
    for axis, dim in sides:
        count = lax.axis_size(axis)
        forward = [(i, i + 1) for i in range(count - 1)]
        backward = [(target, source) for source, target in forward]
        low = lax.ppermute(
            lax.slice_in_dim(block, block.shape[dim] - width, None, axis=dim), axis, forward
        )
        high = lax.ppermute(lax.slice_in_dim(block, 0, width, axis=dim), axis, backward)
        block = jnp.concatenate([low, block, high], axis=dim)
    return block


def match_block(patch_raw, frames, list_y, list_x):
    patch_size = patch_raw.shape[-1]
    cand_count = list_y.shape[-1]
    pixel_count = float(patch_size * patch_size)
    frame_pixels_all = frames.reshape(frames.shape[0], WIN, WIN)

    def crop_all(frame_pixels, shifts_y, shifts_x):

        def crop_one(move_y, move_x):
            return lax.dynamic_slice(
                frame_pixels, (REACH + move_y, REACH + move_x), (patch_size, patch_size)
            )

        return jax.vmap(crop_one)(shifts_y, shifts_x)

    cropped = jax.vmap(crop_all)(frame_pixels_all, list_y, list_x)
    unit_plane = jnp.ones((patch_size, patch_size), patch_raw.dtype)
    patch_sum = jnp.einsum("byx,yx->b", patch_raw, unit_plane, preferred_element_type=jnp.float32)
    patch_square = jnp.einsum(
        "byx,byx->b", patch_raw, patch_raw, preferred_element_type=jnp.float32
    )
    crop_sum = jnp.einsum("bsyx,yx->bs", cropped, unit_plane, preferred_element_type=jnp.float32)
    crop_square = jnp.einsum("bsyx,bsyx->bs", cropped, cropped, preferred_element_type=jnp.float32)
    cross_sum = jnp.einsum("byx,bsyx->bs", patch_raw, cropped, preferred_element_type=jnp.float32)
    patch_mean = patch_sum / pixel_count
    crop_mean = crop_sum / pixel_count
    patch_var = patch_square / pixel_count - patch_mean * patch_mean
    crop_var = crop_square / pixel_count - crop_mean * crop_mean
    cross_mean = cross_sum / pixel_count - patch_mean[:, None] * crop_mean
    correl = cross_mean / jnp.sqrt((patch_var[:, None] + EPSILON) * (crop_var + EPSILON))
    weight = (1.5 + correl) * (1.5 + correl)
    weight_sum = jnp.sum(weight, axis=1)
    along_y = jnp.sum(weight * list_y.astype(jnp.float32), axis=1) / (REACH * weight_sum)
    along_x = jnp.sum(weight * list_x.astype(jnp.float32), axis=1) / (REACH * weight_sum)
    return jnp.stack([along_y, along_x, weight_sum / cand_count])


def match_strip(patch_raw, frames, shift_list, live_count):
    shifts = shift_list.reshape(2, P_SIZE, NS)
    blocks = (live_count + BLK - 1) // BLK

    def one_block(block_index, result):
        block_start = (block_index * BLK).astype(jnp.int32)
        scored = match_block(
            lax.dynamic_slice_in_dim(patch_raw, block_start, BLK, 0),
            lax.dynamic_slice_in_dim(frames, block_start, BLK, 0),
            lax.dynamic_slice_in_dim(shifts[0], block_start, BLK, 0),
            lax.dynamic_slice_in_dim(shifts[1], block_start, BLK, 0),
        )
        return lax.dynamic_update_slice(result, scored, (jnp.zeros((), jnp.int32), block_start))

    result = lax.fori_loop(0, blocks, one_block, jnp.zeros((3, P_SIZE), jnp.float32))
    keeper = (jnp.arange(P_SIZE) < live_count).astype(jnp.float32)
    return result * keeper


def body(patches, windows, candidates, live, edges, stiffness):
    tile_row = lax.axis_index("row")
    tile_col = lax.axis_index("col")
    last_row = lax.axis_size("row") - 1
    last_col = lax.axis_size("col") - 1
    far_east = shifted(windows[0, 0, 0], "col", -1)
    far_south = shifted(windows[0, 0, 1], "row", -1)
    count_east = jnp.where(tile_col < last_col, live[tile_row, tile_col, 0], 0)
    count_south = jnp.where(tile_row < last_row, live[tile_row, tile_col, 1], 0)
    own_east = match_strip(patches[0, 0, 0], far_east, candidates[0, 0, 0], count_east)
    own_south = match_strip(patches[0, 0, 1], far_south, candidates[0, 0, 1], count_south)
    from_west = shifted(own_east, "col", 1)
    from_north = shifted(own_south, "row", 1)
    matches = jnp.stack([own_east, own_south])[None, None]
    slots = jnp.arange(P_SIZE)
    picker = (jnp.arange(GV)[None, :] == (slots * GV // P_SIZE)[:, None]).astype(jnp.float32)
    vertex = jnp.arange(GV * GV)
    incidence = (edges[0, 0][:, None] == vertex[None, :]).astype(jnp.float32) - (
        edges[0, 1][:, None] == vertex[None, :]
    ).astype(jnp.float32)
    spring = stiffness[0]

    def spread(values):
        return jnp.dot(values, picker, precision=PRECISE)

    def sample(values):
        return jnp.dot(values, picker.T, precision=PRECISE)

    conf_east = own_east[2]
    conf_south = own_south[2]
    conf_west = from_west[2]
    conf_north = from_north[2]

    def operate(vector):
        border = with_halo(vector, (("row", 1), ("col", 2)), 1)
        flat_field = vector.reshape(2, GV * GV)
        stretch = jnp.dot(flat_field, incidence.T, precision=PRECISE) * spring
        output = (LAMBDA_REG * flat_field + jnp.dot(stretch, incidence, precision=PRECISE)).reshape(
            2, GV, GV
        )
        output = output.at[:, :, GV - 1].add(
            spread(conf_east * sample(vector[:, :, GV - 1] - border[:, 1:-1, -1]))
        )
        output = output.at[:, :, 0].add(
            spread(conf_west * sample(vector[:, :, 0] - border[:, 1:-1, 0]))
        )
        output = output.at[:, GV - 1, :].add(
            spread(conf_south * sample(vector[:, GV - 1, :] - border[:, -1, 1:-1]))
        )
        output = output.at[:, 0, :].add(
            spread(conf_north * sample(vector[:, 0, :] - border[:, 0, 1:-1]))
        )
        return output

    forcing = jnp.zeros((2, GV, GV), jnp.float32)
    forcing = forcing.at[:, :, GV - 1].add(spread(conf_east * own_east[:2]))
    forcing = forcing.at[:, :, 0].add(-spread(conf_west * from_west[:2]))
    forcing = forcing.at[:, GV - 1, :].add(spread(conf_south * own_south[:2]))
    forcing = forcing.at[:, 0, :].add(-spread(conf_north * from_north[:2]))
    solution = jnp.zeros_like(forcing)
    residual = forcing

    def two_products(values, applied):
        return lax.psum((jnp.sum(values * values), jnp.sum(values * applied)), ("row", "col"))

    applied = operate(residual)
    norm_now, product = two_products(residual, applied)
    step_length = norm_now / product
    direction = residual
    along = applied
    for iteration in range(ITERS):
        solution = solution + step_length * direction
        residual = residual - step_length * along
        if iteration + 1 < ITERS:
            applied = operate(residual)
            norm_next, product = two_products(residual, applied)
            beta_ratio = norm_next / norm_now
            step_length = norm_next / (product - beta_ratio * norm_next / step_length)
            direction = residual + beta_ratio * direction
            along = applied + beta_ratio * along
            norm_now = norm_next
    mesh_shift = solution.reshape(2, GV * GV)[None, None]
    return (matches, mesh_shift)


def solution(mesh):
    return jax.shard_map(
        body,
        mesh=mesh,
        in_specs=(
            P("row", "col", None, None, None, None),
            P("row", "col", None, None, None),
            P("row", "col", None, None, None),
            P(),
            P("row", None, "col"),
            P("row", "col"),
        ),
        out_specs=(P("row", "col", None, None, None), P("row", "col", None, None)),
        check_vma=False,
    )
```

profile of v0, /device:TPU:0, one launch (start us, length us, event | category | flops | bytes accessed | tf_op | source)
XLA Modules:
  0.0 768.7 jit_solution(11452853252674101553)
XLA Ops:
  0.7 2.9 slice_bitcast_fusion.1
  12.0 91.7 %while.49 = (s32[]{:T(128)}, f32[3,16]{1,0:T(4,128)S(1)}, s32[]{:T(128)}, bf16[16,128,128]{2,1,0:T(8,128)(2,1)S(1)}, bf16[16,36864]{1,0:T(8,128)(2,1)}, /*index=...) while((s32[]{:T(128)}, f32[3,16]{1,0:T(4,128)S(1)}, ...), condition=%wide.region_9.10_spmd, body=%wide.region_5.9_spmd.sunk | while | flops 5178357 | bytes 5322758 | solution.py:90
  14.3 87.7 %while.51 = (s32[]{:T(128)}, bf16[4,192,192]{2,1,0:T(8,128)(2,1)S(1)}, s32[32,3]{0,1:T(4,128)S(1)}, bf16[32,128,128]{2,1,0:T(8,128)(2,1)S(1)}, s32[]{:T(128)}) while((s32[]{:T(128)}, bf16[4,192,192]{2,1,0:T(8,128)(2,1)S(1)}, s32[32,3]{0,1:T(4,128)S(1)}, bf16[32,128,128]{2,1,0:T(8,128)(2,1)S(1)}, s32[]{:T(128)}) %tuple.207), condition=%wide.while_cond.17, body=%wide.while_body.17.sunk | while | flops 2 | bytes 65665 | solution.py:48
  15.0 2.0 dynamic-slice_dynamic-update-slice_fusion.4
  17.7 2.0 dynamic-slice_dynamic-update-slice_fusion.4
  20.4 2.0 dynamic-slice_dynamic-update-slice_fusion.4
  23.2 2.0 dynamic-slice_dynamic-update-slice_fusion.4
  25.9 2.0 dynamic-slice_dynamic-update-slice_fusion.4
  28.7 2.0 dynamic-slice_dynamic-update-slice_fusion.4
  31.4 2.0 dynamic-slice_dynamic-update-slice_fusion.4
  34.1 2.0 dynamic-slice_dynamic-update-slice_fusion.4
  36.9 2.0 dynamic-slice_dynamic-update-slice_fusion.4
  39.6 2.0 dynamic-slice_dynamic-update-slice_fusion.4
  42.4 2.0 dynamic-slice_dynamic-update-slice_fusion.4
  45.1 2.0 dynamic-slice_dynamic-update-slice_fusion.4
  47.8 2.0 dynamic-slice_dynamic-update-slice_fusion.4
  50.6 2.0 dynamic-slice_dynamic-update-slice_fusion.4
  53.3 2.0 dynamic-slice_dynamic-update-slice_fusion.4
  56.1 2.0 dynamic-slice_dynamic-update-slice_fusion.4
  58.8 2.0 dynamic-slice_dynamic-update-slice_fusion.4
  61.5 2.0 dynamic-slice_dynamic-update-slice_fusion.4
  64.3 2.0 dynamic-slice_dynamic-update-slice_fusion.4
  67.0 2.0 dynamic-slice_dynamic-update-slice_fusion.4
  69.8 2.0 dynamic-slice_dynamic-update-slice_fusion.4
  72.5 2.0 dynamic-slice_dynamic-update-slice_fusion.4
  75.2 2.0 dynamic-slice_dynamic-update-slice_fusion.4
  78.0 2.0 dynamic-slice_dynamic-update-slice_fusion.4
  80.7 2.0 dynamic-slice_dynamic-update-slice_fusion.4
  83.5 2.0 dynamic-slice_dynamic-update-slice_fusion.4
  86.2 2.0 dynamic-slice_dynamic-update-slice_fusion.4
  88.9 2.0 dynamic-slice_dynamic-update-slice_fusion.4
  91.7 2.0 dynamic-slice_dynamic-update-slice_fusion.4
  94.4 2.0 dynamic-slice_dynamic-update-slice_fusion.4
  97.1 2.0 dynamic-slice_dynamic-update-slice_fusion.4
  99.9 2.0 dynamic-slice_dynamic-update-slice_fusion.4
  103.7 12.8 %collective-permute-start.3 = (f32[3,16]{1,0:T(4,128)S(1)}, f32[3,16]{1,0:T(4,128)S(1)}, u32[]{:S(2)}, u32[]{:S(2)}) collective-permute-start(f32[3,16]{1,0:T(4,128)S(1)} %broadcast_multiply_fusion.2), channel_id=1, source_target_pairs={{0,4},{4,8},{8,12},{12,16},{16,20},{20,24},{24,28},{1,5},{5,9},{9,... | collective-permute-start | bytes 584 | tf_op jit(solution)/shard_map/ppermute | solution.py:23
  116.6 88.6 %while.47 = (s32[]{:T(128)}, f32[3,16]{1,0:T(4,128)S(1)}, s32[]{:T(128)}, bf16[16,128,128]{2,1,0:T(8,128)(2,1)S(1)}, bf16[16,36864]{1,0:T(8,128)(2,1)}, /*index=...) while((s32[]{:T(128)}, f32[3,16]{1,0:T(4,128)S(1)}, ...), condition=%wide.region_4.5_spmd, body=%wide.region_0.4_spmd.sunk | while | flops 5178357 | bytes 5314510 | solution.py:90
  118.5 85.1 %while.50 = (s32[]{:T(128)}, bf16[4,192,192]{2,1,0:T(8,128)(2,1)S(1)}, s32[32,3]{0,1:T(4,128)S(1)}, bf16[32,128,128]{2,1,0:T(8,128)(2,1)S(1)}, s32[]{:T(128)}) while((s32[]{:T(128)}, bf16[4,192,192]{2,1,0:T(8,128)(2,1)S(1)}, s32[32,3]{0,1:T(4,128)S(1)}, bf16[32,128,128]{2,1,0:T(8,128)(2,1)S(1)}, s32[]{:T(128)}) %tuple.210), condition=%wide.while_cond.16, body=%wide.while_body.16.sunk | while | flops 2 | bytes 65665 | solution.py:48
  119.1 2.0 dynamic-slice_dynamic-update-slice_fusion.5
  121.8 2.0 dynamic-slice_dynamic-update-slice_fusion.5
  127.1 2.0 dynamic-slice_dynamic-update-slice_fusion.5
  129.8 2.0 dynamic-slice_dynamic-update-slice_fusion.5
  135.1 2.0 dynamic-slice_dynamic-update-slice_fusion.5
  140.4 2.0 dynamic-slice_dynamic-update-slice_fusion.5
  143.0 2.0 dynamic-slice_dynamic-update-slice_fusion.5
  148.4 2.0 dynamic-slice_dynamic-update-slice_fusion.5
  151.0 2.0 dynamic-slice_dynamic-update-slice_fusion.5
  156.3 2.0 dynamic-slice_dynamic-update-slice_fusion.5
  159.0 2.0 dynamic-slice_dynamic-update-slice_fusion.5
  164.3 2.0 dynamic-slice_dynamic-update-slice_fusion.5
  169.6 2.0 dynamic-slice_dynamic-update-slice_fusion.5
  172.3 2.0 dynamic-slice_dynamic-update-slice_fusion.5
  177.6 2.0 dynamic-slice_dynamic-update-slice_fusion.5
  180.3 2.0 dynamic-slice_dynamic-update-slice_fusion.5
  205.3 174.4 %collective-permute-start.2 = (f32[3,16]{1,0:T(4,128)S(1)}, f32[3,16]{1,0:T(4,128)S(1)}, u32[]{:S(2)}, u32[]{:S(2)}) collective-permute-start(f32[3,16]{1,0:T(4,128)S(1)} %broadcast_multiply_fusion.3), channel_id=1, source_target_pairs={{0,1},{1,2},{2,3},{4,5},{5,6},{6,7},{8,9},{9,10},{10,11},{12,13},{... | collective-permute-start | bytes 584 | tf_op jit(solution)/shard_map/ppermute | solution.py:23
  386.1 13.1 %collective-permute-start.4 = (f32[2,1,16]{1,0,2:T(2,128)S(1)}, f32[2,1,16]{1,0,2:T(2,128)S(1)}, u32[]{:S(2)}, u32[]{:S(2)}) collective-permute-start(f32[2,1,16]{1,0,2:T(2,128)S(1)} %get-tuple-element.515), channel_id=1, source_target_pairs={{0,4},{4,8},{8,12},{12,16},{16,20},{20,24},{24,28},{1,5},{5,9},{9,... | collective-permute-start | bytes 392 | tf_op jit(solution)/shard_map/ppermute | solution.py:31
  401.9 184.5 %collective-permute-start.7 = (f32[2,18,1]{1,0,2:T(2,128)S(1)}, f32[2,18,1]{1,0,2:T(2,128)S(1)}, u32[]{:S(2)}, u32[]{:S(2)}) collective-permute-start(f32[2,18,1]{1,0,2:T(2,128)S(1)} %get-tuple-element.508), channel_id=1, source_target_pairs={{0,1},{1,2},{2,3},{4,5},{5,6},{6,7},{8,9},{9,10},{10,11},{12,13},{... | collective-permute-start | bytes 440 | tf_op jit(solution)/shard_map/ppermute | solution.py:31
  590.2 44.7 %all-reduce.3 = (f32[]{:T(128)}, f32[]{:T(128)}) all-reduce(f32[]{:T(128)} %get-tuple-element.427, f32[]{:T(128)} %get-tuple-element.426), channel_id=1, replica_groups=mesh['row'=8,'col'=4] {'row','col'}, use_global_device_ids=true, to_apply=%region_11.12 | all-reduce | flops 2 | bytes 16 | tf_op jit(solution)/shard_map/psum | solution.py:158
  641.4 2.3 collective-permute-done.9
  645.8 4.8 collective-permute-start.11
  654.6 43.1 %all-reduce.2 = (f32[]{:T(128)}, f32[]{:T(128)}) all-reduce(f32[]{:T(128)} %get-tuple-element.425, f32[]{:T(128)} %get-tuple-element.424), channel_id=1, replica_groups=mesh['row'=8,'col'=4] {'row','col'}, use_global_device_ids=true, to_apply=%region_15.16 | all-reduce | flops 2 | bytes 16 | tf_op jit(solution)/shard_map/psum | solution.py:158
  707.2 3.0 collective-permute-done.13
  712.3 4.8 collective-permute-start.15
  721.0 43.1 %all-reduce.1 = (f32[]{:T(128)}, f32[]{:T(128)}) all-reduce(f32[]{:T(128)} %get-tuple-element.423, f32[]{:T(128)} %get-tuple-element.422), channel_id=1, replica_groups=mesh['row'=8,'col'=4] {'row','col'}, use_global_device_ids=true, to_apply=%region_19.20 | all-reduce | flops 2 | bytes 16 | tf_op jit(solution)/shard_map/psum | solution.py:158
  (348 shorter events, 124.2 us)
Async XLA Ops:
  0.6 8.2 %copy-start.10 = (s32[1,1,2,2,128]{4,3,2,1,0:T(2,128)S(1)}, s32[1,1,2,2,128]{4,3,2,1,0:T(2,128)}, u32[]{:S(2)}) copy-start(s32[1,1,2,2,128]{4,3,2,1,0:T(2,128)} %param.44) | copy-start | bytes 6148
  0.6 8.4 %copy-start.7 = (f32[1,705]{1,0:T(1,128)S(1)}, f32[1,705]{1,0:T(1,128)}, u32[]{:S(2)}) copy-start(f32[1,705]{1,0:T(1,128)} %param.47) | copy-start | bytes 8464
  0.7 10.6 %copy-start.3 = (s32[1,2,705]{2,1,0:T(2,128)S(1)}, s32[1,2,705]{2,1,0:T(2,128)}, u32[]{:S(2)}) copy-start(s32[1,2,705]{2,1,0:T(2,128)} %param.46) | copy-start | bytes 16924
  0.7 11.2 %copy-start = (bf16[1,1,2,16,128,128]{5,4,3,2,1,0:T(8,128)(2,1)S(1)}, bf16[1,1,2,16,128,128]{5,4,3,2,1,0:T(8,128)(2,1)}, u32[]{:S(2)}) copy-start(bf16[1,1,2,16,128,128]{5,4,3,2,1,0:T(8,128)(2,1)} %param.42) | copy-start | bytes 3145732
  3.6 8.4 %collective-permute-start.1 = (bf16[16,36864]{1,0:T(8,128)(2,1)S(1)}, bf16[16,36864]{1,0:T(8,128)(2,1)}, u32[]{:S(2)}, u32[]{:S(2)}) collective-permute-start(bf16[16,36864]{1,0:T(8,128)(2,1)S(1)} %get-tuple-element.501), channel_id=1, source_target_pairs={{4,0},{8,4},{12,8},{16,12},{20,16},{24,20},{28,24},{5,1},{9,5},{13... | collective-permute-start | bytes 3538952 | tf_op jit(solution)/shard_map/ppermute | solution.py:23
  4.9 111.7 %collective-permute-start = (bf16[16,36864]{1,0:T(8,128)(2,1)}, bf16[16,36864]{1,0:T(8,128)(2,1)}, u32[]{:S(2)}, u32[]{:S(2)}) collective-permute-start(bf16[16,36864]{1,0:T(8,128)(2,1)} %get-tuple-element.500), channel_id=1, source_target_pairs={{1,0},{2,1},{3,2},{5,4},{6,5},{7,6},{9,8},{10,9},{11,10},{13,12},{... | collective-permute-start | bytes 3538952 | tf_op jit(solution)/shard_map/ppermute | solution.py:23
  12.0 91.7 %copy-start.8 = (f32[16]{0:T(128)S(1)}, f32[16]{0:T(128)}, u32[]{:S(2)}) copy-start(f32[16]{0:T(128)} %compare_convert_fusion) | copy-start | bytes 196
  12.0 0.6 copy-start.1
  101.9 1.7 copy-start.2
  103.7 277.1 %collective-permute-start.3 = (f32[3,16]{1,0:T(4,128)S(1)}, f32[3,16]{1,0:T(4,128)S(1)}, u32[]{:S(2)}, u32[]{:S(2)}) collective-permute-start(f32[3,16]{1,0:T(4,128)S(1)} %broadcast_multiply_fusion.2), channel_id=1, source_target_pairs={{0,4},{4,8},{8,12},{12,16},{16,20},{20,24},{24,28},{1,5},{5,9},{9,... | collective-permute-start | bytes 584 | tf_op jit(solution)/shard_map/ppermute | solution.py:23
  116.6 88.7 %copy-start.9 = (f32[16]{0:T(128)S(1)}, f32[16]{0:T(128)}, u32[]{:S(2)}) copy-start(f32[16]{0:T(128)} %compare_convert_fusion.1) | copy-start | bytes 196
  116.6 263.2 %copy-start.11 = (s32[16]{0:T(128)S(1)}, s32[16]{0:T(128)}, u32[]{:S(2)}) copy-start(s32[16]{0:T(128)} %and_select_fusion) | copy-start | bytes 196
  116.6 267.7 %copy-start.4 = (s32[705]{0:T(1024)S(1)}, s32[705]{0:T(1024)}, u32[]{:S(2)}) copy-start(s32[705]{0:T(1024)} %get-tuple-element.428) | copy-start | bytes 8464
  116.6 267.7 %copy-start.5 = (s32[705]{0:T(1024)S(1)}, s32[705]{0:T(1024)}, u32[]{:S(2)}) copy-start(s32[705]{0:T(1024)} %get-tuple-element.429) | copy-start | bytes 8464
  116.6 267.7 %copy-start.6 = (f32[705]{0:T(1024)S(1)}, f32[705]{0:T(1024)}, u32[]{:S(2)}) copy-start(f32[705]{0:T(1024)} %reduce.44) | copy-start | bytes 8464
  205.3 175.9 %collective-permute-start.2 = (f32[3,16]{1,0:T(4,128)S(1)}, f32[3,16]{1,0:T(4,128)S(1)}, u32[]{:S(2)}, u32[]{:S(2)}) collective-permute-start(f32[3,16]{1,0:T(4,128)S(1)} %broadcast_multiply_fusion.3), channel_id=1, source_target_pairs={{0,1},{1,2},{2,3},{4,5},{5,6},{6,7},{8,9},{9,10},{10,11},{12,13},{... | collective-permute-start | bytes 584 | tf_op jit(solution)/shard_map/ppermute | solution.py:23
  382.7 3.3 collective-permute-start.5
  386.1 13.9 %collective-permute-start.4 = (f32[2,1,16]{1,0,2:T(2,128)S(1)}, f32[2,1,16]{1,0,2:T(2,128)S(1)}, u32[]{:S(2)}, u32[]{:S(2)}) collective-permute-start(f32[2,1,16]{1,0,2:T(2,128)S(1)} %get-tuple-element.515), channel_id=1, source_target_pairs={{0,4},{4,8},{8,12},{12,16},{16,20},{20,24},{24,28},{1,5},{5,9},{9,... | collective-permute-start | bytes 392 | tf_op jit(solution)/shard_map/ppermute | solution.py:31
  400.7 185.8 %collective-permute-start.6 = (f32[2,18,1]{1,0,2:T(2,128)S(1)}, f32[2,18,1]{1,0,2:T(2,128)S(1)}, u32[]{:S(2)}, u32[]{:S(2)}) collective-permute-start(f32[2,18,1]{1,0,2:T(2,128)S(1)} %get-tuple-element.509), channel_id=1, source_target_pairs={{1,0},{2,1},{3,2},{5,4},{6,5},{7,6},{9,8},{10,9},{11,10},{13,12},{... | collective-permute-start | bytes 440 | tf_op jit(solution)/shard_map/ppermute | solution.py:34
  401.9 185.8 %collective-permute-start.7 = (f32[2,18,1]{1,0,2:T(2,128)S(1)}, f32[2,18,1]{1,0,2:T(2,128)S(1)}, u32[]{:S(2)}, u32[]{:S(2)}) collective-permute-start(f32[2,18,1]{1,0,2:T(2,128)S(1)} %get-tuple-element.508), channel_id=1, source_target_pairs={{0,1},{1,2},{2,3},{4,5},{5,6},{6,7},{8,9},{9,10},{10,11},{12,13},{... | collective-permute-start | bytes 440 | tf_op jit(solution)/shard_map/ppermute | solution.py:31
  636.5 3.0 collective-permute-start.8
  639.8 3.9 collective-permute-start.9
  644.5 6.1 collective-permute-start.10
  645.8 6.1 collective-permute-start.11
  702.3 3.0 collective-permute-start.12
  705.7 4.6 collective-permute-start.13
  711.0 6.1 collective-permute-start.14
  712.3 6.1 collective-permute-start.15
where the time goes:
time: 775 us; the launch traced here: 769 us
  starting transfers between devices  407 us (53%)
  local copies, waits for them, and re-layouts  191 us (25%)
  blocking collectives  131 us (17%)
  between operations  12.4 us (2%)
  matrix products  9.82 us (1%)
  other arithmetic  8.31 us (1%)
  waiting for transfers between devices  8.25 us (1%)
    ppermute x6, starting transfers between devices, with_halo(): lax.ppermute(lax.slice_in_dim(block, block.shape[dim] - width, None, axis...  210 us
    ppermute x4, starting transfers between devices, shifted(): return lax.ppermute(x, axis, pairs)  190 us
    gather x192, local copies, waits for them, and re-layouts  172 us
    psum x3, blocking collectives, two_products(): lax.psum((jnp.sum(values * values), jnp.sum(values * applied)), ('row', '...  131 us
  transfers between devices with their start and end apart: 16, of which 6 were waited for; matrix products, arithmetic and copies ran while one was open for 25% of the time, Pallas kernels for 0%

commit v1 on v0

--- a/solution.py
+++ b/solution.py
@@ -1,13 +1,14 @@
 import jax
 import jax.numpy as jnp
 from jax import lax
+from jax.experimental import pallas as pl
+from jax.experimental.pallas import tpu as pltpu
 from jax.sharding import PartitionSpec as P
 
 REACH = 32
 WIN = 192
 NS = 8
 P_SIZE = 16
-BLK = 4
 GV = 16
 ITERS = 3
 
@@ -36,75 +37,136 @@
     return block
 
 
-def match_block(patch_raw, frames, list_y, list_x):
-    patch_size = patch_raw.shape[-1]
-    cand_count = list_y.shape[-1]
+def match_kernel(counts, cands, cand_rows, west, north, frames, out, flat, plane, sums):
+    patch_size = west.shape[-1]
+    chunks = frames.shape[-1] // 128
+    pitch = chunks + 1
+    half = patch_size // 2
+    lane = lax.broadcasted_iota(jnp.int32, (half, 128), 1)
     pixel_count = float(patch_size * patch_size)
-    frame_pixels_all = frames.reshape(frames.shape[0], WIN, WIN)
-
-    def crop_all(frame_pixels, shifts_y, shifts_x):
-
-        def crop_one(move_y, move_x):
-            return lax.dynamic_slice(
-                frame_pixels, (REACH + move_y, REACH + move_x), (patch_size, patch_size)
-            )
-
-        return jax.vmap(crop_one)(shifts_y, shifts_x)
-
-    cropped = jax.vmap(crop_all)(frame_pixels_all, list_y, list_x)
-    unit_plane = jnp.ones((patch_size, patch_size), patch_raw.dtype)
-    patch_sum = jnp.einsum("byx,yx->b", patch_raw, unit_plane, preferred_element_type=jnp.float32)
-    patch_square = jnp.einsum(
-        "byx,byx->b", patch_raw, patch_raw, preferred_element_type=jnp.float32
-    )
-    crop_sum = jnp.einsum("bsyx,yx->bs", cropped, unit_plane, preferred_element_type=jnp.float32)
-    crop_square = jnp.einsum("bsyx,bsyx->bs", cropped, cropped, preferred_element_type=jnp.float32)
-    cross_sum = jnp.einsum("byx,bsyx->bs", patch_raw, cropped, preferred_element_type=jnp.float32)
-    patch_mean = patch_sum / pixel_count
-    crop_mean = crop_sum / pixel_count
-    patch_var = patch_square / pixel_count - patch_mean * patch_mean
-    crop_var = crop_square / pixel_count - crop_mean * crop_mean
-    cross_mean = cross_sum / pixel_count - patch_mean[:, None] * crop_mean
-    correl = cross_mean / jnp.sqrt((patch_var[:, None] + EPSILON) * (crop_var + EPSILON))
-    weight = (1.5 + correl) * (1.5 + correl)
-    weight_sum = jnp.sum(weight, axis=1)
-    along_y = jnp.sum(weight * list_y.astype(jnp.float32), axis=1) / (REACH * weight_sum)
-    along_x = jnp.sum(weight * list_x.astype(jnp.float32), axis=1) / (REACH * weight_sum)
-    return jnp.stack([along_y, along_x, weight_sum / cand_count])
-
-
-def match_strip(patch_raw, frames, shift_list, live_count):
-    shifts = shift_list.reshape(2, P_SIZE, NS)
-    blocks = (live_count + BLK - 1) // BLK
-
-    def one_block(block_index, result):
-        block_start = (block_index * BLK).astype(jnp.int32)
-        scored = match_block(
-            lax.dynamic_slice_in_dim(patch_raw, block_start, BLK, 0),
-            lax.dynamic_slice_in_dim(frames, block_start, BLK, 0),
-            lax.dynamic_slice_in_dim(shifts[0], block_start, BLK, 0),
-            lax.dynamic_slice_in_dim(shifts[1], block_start, BLK, 0),
-        )
-        return lax.dynamic_update_slice(result, scored, (jnp.zeros((), jnp.int32), block_start))
-
-    result = lax.fori_loop(0, blocks, one_block, jnp.zeros((3, P_SIZE), jnp.float32))
-    keeper = (jnp.arange(P_SIZE) < live_count).astype(jnp.float32)
-    return result * keeper
+
+    def fold(values):
+        return jnp.sum(values.reshape(half // 8, 8, 128), axis=0)
+
+    for seam in range(2):
+        patches = (west, north)[seam]
+
+        def spread_chunk(chunk, carry):
+            start = pl.multiple_of(chunk * 128, 128)
+            piece = frames[seam, :, pl.ds(start, 128)].astype(jnp.float32)
+            flat[pl.ds(chunk, P_SIZE, stride=pitch), :] = piece
+            return carry
+
+        lax.fori_loop(0, chunks, spread_chunk, 0, unroll=8)
+
+        def one_patch(slot, carry):
+            plane[...] = patches[slot].astype(jnp.float32)
+            parts = [plane[pl.ds(parity, half, stride=2), :] for parity in range(2)]
+            own_sum = fold(parts[0] + parts[1])
+            own_square = fold(parts[0] * parts[0] + parts[1] * parts[1])
+            for cand in range(NS):
+                index = slot * NS + cand
+                row = REACH + cands[seam, 0, index]
+                col = REACH + cands[seam, 1, index]
+                crop_sum = crop_square = cross_sum = 0.0
+                for parity in range(2):
+                    place = (row + parity) * WIN + col
+                    chunk = slot * pitch + lax.shift_right_logical(place, 7)
+                    offset = lax.bitwise_and(place, 127)
+                    low = flat[pl.ds(chunk, half, stride=3), :]
+                    high = flat[pl.ds(chunk + 1, half, stride=3), :]
+                    crop = jnp.where(lane >= offset, low, high)
+                    patch = pltpu.roll(plane[pl.ds(parity, half, stride=2), :], offset, 1)
+                    crop_sum = crop_sum + fold(crop)
+                    crop_square = crop_square + fold(crop * crop)
+                    cross_sum = cross_sum + fold(crop * patch)
+                spot = pl.ds(pl.multiple_of(index * 8, 8), 8)
+                sums[0, spot, :] = crop_sum
+                sums[1, spot, :] = crop_square
+                sums[2, spot, :] = cross_sum
+                sums[3, spot, :] = own_sum
+                sums[4, spot, :] = own_square
+            return carry
+
+        lax.fori_loop(0, counts[seam], one_patch, 0)
+
+        def total(which):
+            values = sums[which, pl.ds(0, P_SIZE * NS, stride=8), :]
+            for part in range(1, 8):
+                values = values + sums[which, pl.ds(part, P_SIZE * NS, stride=8), :]
+            return jnp.sum(values.T, axis=0, keepdims=True) / pixel_count
+
+        crop_mean, crop_square, cross_mean, patch_mean, patch_square = [total(n) for n in range(5)]
+        patch_var = patch_square - patch_mean * patch_mean
+        crop_var = crop_square - crop_mean * crop_mean
+        cross = cross_mean - patch_mean * crop_mean
+        correl = cross / jnp.sqrt((patch_var + EPSILON) * (crop_var + EPSILON))
+        weight = (1.5 + correl) * (1.5 + correl)
+        index = lax.broadcasted_iota(jnp.int32, weight.shape, 1)
+        weight = jnp.where(index < counts[seam] * NS, weight, 0.0)
+        rows = jnp.concatenate(
+            [
+                weight * cand_rows[seam, 0:1, :].astype(jnp.float32),
+                weight * cand_rows[seam, 1:2, :].astype(jnp.float32),
+                weight,
+                jnp.zeros((5, P_SIZE * NS), jnp.float32),
+            ],
+            axis=0,
+        )
+        group = lax.broadcasted_iota(jnp.int32, (P_SIZE * NS, P_SIZE), 0) // NS
+        member = lax.broadcasted_iota(jnp.int32, (P_SIZE * NS, P_SIZE), 1)
+        gathered = jnp.dot(
+            rows, (group == member).astype(jnp.float32), precision=PRECISE,
+            preferred_element_type=jnp.float32,
+        )
+        weight_sum = gathered[2:3]
+        result = jnp.concatenate(
+            [gathered[0:2] / (REACH * weight_sum), weight_sum / NS], axis=0
+        )
+        slot = lax.broadcasted_iota(jnp.int32, result.shape, 1)
+        out[seam] = jnp.where(slot < counts[seam], result, 0.0)
+
+
+def match_call(counts, cands, west, north, frames):
+    patch_size = west.shape[-1]
+    pitch = frames.shape[-1] // 128 + 1
+    smem = pl.BlockSpec(memory_space=pltpu.SMEM)
+    vmem = pl.BlockSpec(memory_space=pltpu.VMEM)
+    return pl.pallas_call(
+        match_kernel,
+        out_shape=jax.ShapeDtypeStruct((2, 3, P_SIZE), jnp.float32),
+        in_specs=[smem, smem, vmem, vmem, vmem, vmem],
+        out_specs=vmem,
+        scratch_shapes=[
+            pltpu.VMEM((P_SIZE * pitch, 128), jnp.float32),
+            pltpu.VMEM((patch_size, patch_size), jnp.float32),
+            pltpu.VMEM((5, P_SIZE * NS * 8, 128), jnp.float32),
+        ],
+        compiler_params=pltpu.CompilerParams(vmem_limit_bytes=40 * 1024 * 1024),
+        name="match",
+    )(counts, cands, cands, west, north, frames)
 
 
 def body(patches, windows, candidates, live, edges, stiffness):
     tile_row = lax.axis_index("row")
     tile_col = lax.axis_index("col")
-    last_row = lax.axis_size("row") - 1
-    last_col = lax.axis_size("col") - 1
-    far_east = shifted(windows[0, 0, 0], "col", -1)
-    far_south = shifted(windows[0, 0, 1], "row", -1)
-    count_east = jnp.where(tile_col < last_col, live[tile_row, tile_col, 0], 0)
-    count_south = jnp.where(tile_row < last_row, live[tile_row, tile_col, 1], 0)
-    own_east = match_strip(patches[0, 0, 0], far_east, candidates[0, 0, 0], count_east)
-    own_south = match_strip(patches[0, 0, 1], far_south, candidates[0, 0, 1], count_south)
-    from_west = shifted(own_east, "col", 1)
-    from_north = shifted(own_south, "row", 1)
+    west_patches = shifted(patches[0, 0, 0], "col", 1)
+    north_patches = shifted(patches[0, 0, 1], "row", 1)
+    west_cands = shifted(candidates[0, 0, 0], "col", 1)
+    north_cands = shifted(candidates[0, 0, 1], "row", 1)
+    count_west = jnp.where(tile_col > 0, live[tile_row, jnp.maximum(tile_col - 1, 0), 0], 0)
+    count_north = jnp.where(tile_row > 0, live[jnp.maximum(tile_row - 1, 0), tile_col, 1], 0)
+    scored = match_call(
+        jnp.stack([count_west, count_north]),
+        jnp.stack([west_cands, north_cands]),
+        west_patches,
+        north_patches,
+        windows[0, 0],
+    )
+    from_west = scored[0]
+    from_north = scored[1]
+    own_east = shifted(from_west, "col", -1)
+    own_south = shifted(from_north, "row", -1)
     matches = jnp.stack([own_east, own_south])[None, None]
     slots = jnp.arange(P_SIZE)
     picker = (jnp.arange(GV)[None, :] == (slots * GV // P_SIZE)[:, None]).astype(jnp.float32)

time: 775 us -> 233 us (0.30)
  starting transfers between devices: 407 us -> 45.8 us
  local copies, waits for them, and re-layouts: 191 us -> 15 us
    ppermute x6, starting transfers between devices: 210 us -> 22 us  [with_halo(): lax.ppermute(lax.slice_in_dim(block, block.shape[dim] - width, None, axis...]
    ppermute x4 -> x6, starting transfers between devices: 190 us -> 16.1 us  [shifted(): return lax.ppermute(x, axis, pairs)]
    gather x194 -> x0, local copies, waits for them, and re-layouts: 172 us -> none
  transfers between devices with their start and end apart: 16 -> 18, of which waited for: 6 -> 9; matrix products, arithmetic and copies ran while one was open for 25% -> 5% of each run, Pallas kernels for 0% -> 0%
where the time goes in v1:
time: 233 us; the launch traced here: 232 us
  blocking collectives  131 us (56%)
  starting transfers between devices  45.8 us (20%)
  local copies, waits for them, and re-layouts  15 us (6%)
  between operations  12.2 us (5%)
  waiting for transfers between devices  11.9 us (5%)
  matrix products  9.83 us (4%)
  other arithmetic  3.82 us (2%)
  Pallas kernels  2.86 us (1%)
    psum x3, blocking collectives, two_products(): lax.psum((jnp.sum(values * values), jnp.sum(values * applied)), ('row', '...  131 us
    ppermute x6, starting transfers between devices, with_halo(): lax.ppermute(lax.slice_in_dim(block, block.shape[dim] - width, None, axis...  22 us
    ppermute x6, starting transfers between devices, shifted(): return lax.ppermute(x, axis, pairs)  16.1 us
    ppermute x6, starting transfers between devices, with_halo(): lax.ppermute(lax.slice_in_dim(block, 0, width, axis=dim), axis, backward)  7.74 us
    ppermute x6, waiting for transfers between devices, with_halo(): lax.ppermute(lax.slice_in_dim(block, 0, width, axis=dim), axis, backward)  6.58 us
  transfers between devices with their start and end apart: 18, of which 9 were waited for; matrix products, arithmetic and copies ran while one was open for 5% of the time, Pallas kernels for 0%

profile of v1, /device:TPU:0, one launch (start us, length us, event | category | flops | bytes accessed | tf_op | source)
XLA Modules:
  0.0 232.4 jit_solution(16083652544733012646)
XLA Ops:
  0.6 1.3 slice_bitcast_fusion
  1.9 4.9 %collective-permute-start.2 = (bf16[16,128,128]{2,1,0:T(8,128)(2,1)S(1)}, bf16[16,128,128]{2,1,0:T(8,128)(2,1)S(1)}, u32[]{:S(2)}, u32[]{:S(2)}) collective-permute-start(bf16[16,128,128]{2,1,0:T(8,128)(2,1)S(1)} %get-tuple-element.209), channel_id=1, source_target_pairs={{0,1},{1,2},{2,3},{4,5},{5,6},{6,7},{8,9},{9,10},{10,11},{12,13},{... | collective-permute-start | bytes 1572872 | tf_op jit(solution)/shard_map/ppermute | solution.py:24
  6.8 1.5 collective-permute-start.3
  8.3 0.7 slice_bitcast_fusion.7
  9.0 3.4 %collective-permute-start = (s32[2,128]{1,0:T(2,128)S(1)}, s32[2,128]{1,0:T(2,128)S(1)}, u32[]{:S(2)}, u32[]{:S(2)}) collective-permute-start(s32[2,128]{1,0:T(2,128)S(1)} %get-tuple-element.228), channel_id=1, source_target_pairs={{0,1},{1,2},{2,3},{4,5},{5,6},{6,7},{8,9},{9,10},{10,11},{12,13},{... | collective-permute-start | bytes 3080 | tf_op jit(solution)/shard_map/ppermute | solution.py:24
  12.4 3.7 %collective-permute-start.1 = (s32[2,128]{1,0:T(2,128)S(1)}, s32[2,128]{1,0:T(2,128)S(1)}, u32[]{:S(2)}, u32[]{:S(2)}) collective-permute-start(s32[2,128]{1,0:T(2,128)S(1)} %get-tuple-element.229), channel_id=1, source_target_pairs={{0,4},{4,8},{8,12},{12,16},{16,20},{20,24},{24,28},{1,5},{5,9},{9,... | collective-permute-start | bytes 3080 | tf_op jit(solution)/shard_map/ppermute | solution.py:24
  16.1 1.3 constant_dynamic-slice_fusion
  18.8 0.8 slice_reduce_fusion.1
  19.7 0.7 reduce.34
  20.4 1.7 copy-done
  22.1 2.9 %match.1 = f32[2,3,16]{2,1,0:T(4,128)S(1)} custom-call(s32[2]{0:T(128)S(1)} %pad_add_fusion.1.counts, s32[2,2,128]{2,1,0:T(2,128)S(1)} %pad_add_fusion.cands.cand_rows, s32[2,2,128]{2,1,0:T(2,128)S(1)} %pad_add_fusion.cands.cand_rows, bf16[16,128,128]{2,1,0:T(8,128)(2,1)S(1)} %collective-permute-done.2.west, ...), custom_call_target="tpu_custom_call" | custom-call | tf_op jit(solution)/shard_map/match/pallas_call | solution.py:135
  25.0 1.3 collective-permute-start.4
  26.3 1.3 collective-permute-start.5
  27.9 1.8 collective-permute-done.5
  29.9 0.6 collective-permute-done.4
  30.7 0.2 fusion.14
  31.0 1.2 scatter-add.56
  32.3 1.3 collective-permute-start.7
  33.9 0.9 convolution_multiply_fusion.2
  34.7 0.6 convolution_add_fusion.2
  35.5 0.6 copy.58
  36.1 0.5 collective-permute-done.7
  36.7 4.4 %collective-permute-start.6 = (f32[2,1,16]{1,0,2:T(2,128)S(1)}, f32[2,1,16]{1,0,2:T(2,128)S(1)}, u32[]{:S(2)}, u32[]{:S(2)}) collective-permute-start(f32[2,1,16]{1,0,2:T(2,128)S(1)} %get-tuple-element.221), channel_id=1, source_target_pairs={{0,4},{4,8},{8,12},{12,16},{16,20},{20,24},{24,28},{1,5},{5,9},{9,... | collective-permute-start | bytes 392 | tf_op jit(solution)/shard_map/ppermute | solution.py:32
  41.4 0.2 convolution_bitcast_fusion.9
  41.7 0.2 collective-permute-done.6
  42.0 0.2 convolution_multiply_fusion.11
  42.2 0.2 convolution_bitcast_fusion.8
  42.6 1.3 collective-permute-start.8
  43.9 5.4 %collective-permute-start.9 = (f32[2,18,1]{1,0,2:T(2,128)S(1)}, f32[2,18,1]{1,0,2:T(2,128)S(1)}, u32[]{:S(2)}, u32[]{:S(2)}) collective-permute-start(f32[2,18,1]{1,0,2:T(2,128)S(1)} %get-tuple-element.214), channel_id=1, source_target_pairs={{0,1},{1,2},{2,3},{4,5},{5,6},{6,7},{8,9},{9,10},{10,11},{12,13},{... | collective-permute-start | bytes 440 | tf_op jit(solution)/shard_map/ppermute | solution.py:32
  49.5 0.2 fusion.11
  49.7 0.9 collective-permute-done.9
  50.8 0.2 fusion.9
  51.1 1.2 scatter-add.64
  52.5 0.7 multiply_reduce_fusion.4
  53.2 45.0 %all-reduce.3 = (f32[]{:T(128)}, f32[]{:T(128)}) all-reduce(f32[]{:T(128)} %get-tuple-element.199, f32[]{:T(128)} %get-tuple-element.198), channel_id=1, replica_groups=mesh['row'=8,'col'=4] {'row','col'}, use_global_device_ids=true, to_apply=%region_1.2 | all-reduce | flops 2 | bytes 16 | tf_op jit(solution)/shard_map/psum | solution.py:220
  99.7 1.3 collective-permute-start.10
  101.0 0.8 convolution_multiply_fusion.1
  101.9 0.6 convolution_add_fusion.1
  103.0 1.3 collective-permute-start.11
  104.6 3.9 %collective-permute-done.11 = f32[2,1,16]{1,0,2:T(2,128)S(1)} collective-permute-done((f32[2,1,16]{1,0,2:T(2,128)S(1)}, f32[2,1,16]{1,0,2:T(2,128)S(1)}, u32[]{:S(2)}, u32[]{:S(2)}) %collective-permute-start.11) | collective-permute-done | bytes 160 | tf_op jit(solution)/shard_map/ppermute | solution.py:35
  108.8 0.2 convolution_bitcast_fusion.5
  109.2 1.3 collective-permute-start.12
  110.5 4.8 %collective-permute-start.13 = (f32[2,18,1]{1,0,2:T(2,128)S(1)}, f32[2,18,1]{1,0,2:T(2,128)S(1)}, u32[]{:S(2)}, u32[]{:S(2)}) collective-permute-start(f32[2,18,1]{1,0,2:T(2,128)S(1)} %get-tuple-element.212), channel_id=1, source_target_pairs={{0,1},{1,2},{2,3},{4,5},{5,6},{6,7},{8,9},{9,10},{10,11},{12,13},{... | collective-permute-start | bytes 440 | tf_op jit(solution)/shard_map/ppermute | solution.py:32
  115.5 0.2 fusion.7
  115.7 0.9 collective-permute-done.13
  116.8 0.2 fusion.5
  117.1 1.2 scatter-add.70
  118.5 0.6 multiply_reduce_fusion.2
  119.1 43.0 %all-reduce.2 = (f32[]{:T(128)}, f32[]{:T(128)}) all-reduce(f32[]{:T(128)} %get-tuple-element.197, f32[]{:T(128)} %get-tuple-element.196), channel_id=1, replica_groups=mesh['row'=8,'col'=4] {'row','col'}, use_global_device_ids=true, to_apply=%region_5.6 | all-reduce | flops 2 | bytes 16 | tf_op jit(solution)/shard_map/psum | solution.py:220
  166.8 1.3 collective-permute-start.14
  168.2 0.8 convolution_multiply_fusion
  169.1 0.6 convolution_add_fusion
  170.2 1.3 collective-permute-start.15
  171.8 2.2 collective-permute-done.15
  174.4 0.2 convolution_bitcast_fusion.1
  174.8 1.3 collective-permute-start.16
  176.1 4.8 %collective-permute-start.17 = (f32[2,18,1]{1,0,2:T(2,128)S(1)}, f32[2,18,1]{1,0,2:T(2,128)S(1)}, u32[]{:S(2)}, u32[]{:S(2)}) collective-permute-start(f32[2,18,1]{1,0,2:T(2,128)S(1)} %get-tuple-element.210), channel_id=1, source_target_pairs={{0,1},{1,2},{2,3},{4,5},{5,6},{6,7},{8,9},{9,10},{10,11},{12,13},{... | collective-permute-start | bytes 440 | tf_op jit(solution)/shard_map/ppermute | solution.py:32
  181.1 0.2 fusion.3
  181.3 0.9 collective-permute-done.17
  182.3 0.2 fusion.1
  182.7 1.2 scatter-add.76
  184.0 0.7 multiply_reduce_fusion
  184.7 43.0 %all-reduce.1 = (f32[]{:T(128)}, f32[]{:T(128)}) all-reduce(f32[]{:T(128)} %get-tuple-element.195, f32[]{:T(128)} %get-tuple-element.194), channel_id=1, replica_groups=mesh['row'=8,'col'=4] {'row','col'}, use_global_device_ids=true, to_apply=%region_9.10 | all-reduce | flops 2 | bytes 16 | tf_op jit(solution)/shard_map/psum | solution.py:220
  231.7 0.7 broadcast_in_dim_reshape.3
  (88 shorter events, 7.3 us)
Async XLA Ops:
  1.9 18.5 %collective-permute-start.2 = (bf16[16,128,128]{2,1,0:T(8,128)(2,1)S(1)}, bf16[16,128,128]{2,1,0:T(8,128)(2,1)S(1)}, u32[]{:S(2)}, u32[]{:S(2)}) collective-permute-start(bf16[16,128,128]{2,1,0:T(8,128)(2,1)S(1)} %get-tuple-element.209), channel_id=1, source_target_pairs={{0,1},{1,2},{2,3},{4,5},{5,6},{6,7},{8,9},{9,10},{10,11},{12,13},{... | collective-permute-start | bytes 1572872 | tf_op jit(solution)/shard_map/ppermute | solution.py:24
  6.8 13.6 %collective-permute-start.3 = (bf16[16,128,128]{2,1,0:T(8,128)(2,1)S(1)}, bf16[16,128,128]{2,1,0:T(8,128)(2,1)S(1)}, u32[]{:S(2)}, u32[]{:S(2)}) collective-permute-start(bf16[16,128,128]{2,1,0:T(8,128)(2,1)S(1)} %get-tuple-element.208), channel_id=1, source_target_pairs={{0,4},{4,8},{8,12},{12,16},{16,20},{20,24},{24,28},{1,5},{5,9},{9,... | collective-permute-start | bytes 1572872 | tf_op jit(solution)/shard_map/ppermute | solution.py:24
  9.0 11.4 %collective-permute-start = (s32[2,128]{1,0:T(2,128)S(1)}, s32[2,128]{1,0:T(2,128)S(1)}, u32[]{:S(2)}, u32[]{:S(2)}) collective-permute-start(s32[2,128]{1,0:T(2,128)S(1)} %get-tuple-element.228), channel_id=1, source_target_pairs={{0,1},{1,2},{2,3},{4,5},{5,6},{6,7},{8,9},{9,10},{10,11},{12,13},{... | collective-permute-start | bytes 3080 | tf_op jit(solution)/shard_map/ppermute | solution.py:24
  12.4 8.0 %collective-permute-start.1 = (s32[2,128]{1,0:T(2,128)S(1)}, s32[2,128]{1,0:T(2,128)S(1)}, u32[]{:S(2)}, u32[]{:S(2)}) collective-permute-start(s32[2,128]{1,0:T(2,128)S(1)} %get-tuple-element.229), channel_id=1, source_target_pairs={{0,4},{4,8},{8,12},{12,16},{16,20},{20,24},{24,28},{1,5},{5,9},{9,... | collective-permute-start | bytes 3080 | tf_op jit(solution)/shard_map/ppermute | solution.py:24
  20.4 1.7 copy-start
  25.0 5.6 %collective-permute-start.4 = (f32[3,16]{1,0:T(4,128)S(1)}, f32[3,16]{1,0:T(4,128)S(1)}, u32[]{:S(2)}, u32[]{:S(2)}) collective-permute-start(f32[3,16]{1,0:T(4,128)S(1)} %get-tuple-element.224), channel_id=1, source_target_pairs={{1,0},{2,1},{3,2},{5,4},{6,5},{7,6},{9,8},{10,9},{11,10},{13,12},{... | collective-permute-start | bytes 584 | tf_op jit(solution)/shard_map/ppermute | solution.py:24
  26.3 3.3 %collective-permute-start.5 = (f32[3,16]{1,0:T(4,128)S(1)}, f32[3,16]{1,0:T(4,128)S(1)}, u32[]{:S(2)}, u32[]{:S(2)}) collective-permute-start(f32[3,16]{1,0:T(4,128)S(1)} %get-tuple-element.225), channel_id=1, source_target_pairs={{4,0},{8,4},{12,8},{16,12},{20,16},{24,20},{28,24},{5,1},{9,5},{13... | collective-permute-start | bytes 584 | tf_op jit(solution)/shard_map/ppermute | solution.py:24
  32.3 4.3 %collective-permute-start.7 = (f32[2,1,16]{1,0,2:T(2,128)S(1)}, f32[2,1,16]{1,0,2:T(2,128)S(1)}, u32[]{:S(2)}, u32[]{:S(2)}) collective-permute-start(f32[2,1,16]{1,0,2:T(2,128)S(1)} %slice_add_fusion.6), channel_id=1, source_target_pairs={{4,0},{8,4},{12,8},{16,12},{20,16},{24,20},{28,24},{5,1},{9,5},{13... | collective-permute-start | bytes 392 | tf_op jit(solution)/shard_map/ppermute | solution.py:35
  36.7 5.2 %collective-permute-start.6 = (f32[2,1,16]{1,0,2:T(2,128)S(1)}, f32[2,1,16]{1,0,2:T(2,128)S(1)}, u32[]{:S(2)}, u32[]{:S(2)}) collective-permute-start(f32[2,1,16]{1,0,2:T(2,128)S(1)} %get-tuple-element.221), channel_id=1, source_target_pairs={{0,4},{4,8},{8,12},{12,16},{16,20},{20,24},{24,28},{1,5},{5,9},{9,... | collective-permute-start | bytes 392 | tf_op jit(solution)/shard_map/ppermute | solution.py:32
  42.6 6.7 %collective-permute-start.8 = (f32[2,18,1]{1,0,2:T(2,128)S(1)}, f32[2,18,1]{1,0,2:T(2,128)S(1)}, u32[]{:S(2)}, u32[]{:S(2)}) collective-permute-start(f32[2,18,1]{1,0,2:T(2,128)S(1)} %get-tuple-element.215), channel_id=1, source_target_pairs={{1,0},{2,1},{3,2},{5,4},{6,5},{7,6},{9,8},{10,9},{11,10},{13,12},{... | collective-permute-start | bytes 440 | tf_op jit(solution)/shard_map/ppermute | solution.py:35
  43.9 6.7 %collective-permute-start.9 = (f32[2,18,1]{1,0,2:T(2,128)S(1)}, f32[2,18,1]{1,0,2:T(2,128)S(1)}, u32[]{:S(2)}, u32[]{:S(2)}) collective-permute-start(f32[2,18,1]{1,0,2:T(2,128)S(1)} %get-tuple-element.214), channel_id=1, source_target_pairs={{0,1},{1,2},{2,3},{4,5},{5,6},{6,7},{8,9},{9,10},{10,11},{12,13},{... | collective-permute-start | bytes 440 | tf_op jit(solution)/shard_map/ppermute | solution.py:32
  99.7 3.0 %collective-permute-start.10 = (f32[2,1,16]{1,0,2:T(2,128)S(1)}, f32[2,1,16]{1,0,2:T(2,128)S(1)}, u32[]{:S(2)}, u32[]{:S(2)}) collective-permute-start(f32[2,1,16]{1,0,2:T(2,128)S(1)} %slice.555), channel_id=1, source_target_pairs={{0,4},{4,8},{8,12},{12,16},{16,20},{20,24},{24,28},{1,5},{5,9},{9,... | collective-permute-start | bytes 392 | tf_op jit(solution)/shard_map/ppermute | solution.py:32
  103.0 5.4 %collective-permute-start.11 = (f32[2,1,16]{1,0,2:T(2,128)S(1)}, f32[2,1,16]{1,0,2:T(2,128)S(1)}, u32[]{:S(2)}, u32[]{:S(2)}) collective-permute-start(f32[2,1,16]{1,0,2:T(2,128)S(1)} %get-tuple-element.219), channel_id=1, source_target_pairs={{4,0},{8,4},{12,8},{16,12},{20,16},{24,20},{28,24},{5,1},{9,5},{13... | collective-permute-start | bytes 392 | tf_op jit(solution)/shard_map/ppermute | solution.py:35
  109.2 6.1 %collective-permute-start.12 = (f32[2,18,1]{1,0,2:T(2,128)S(1)}, f32[2,18,1]{1,0,2:T(2,128)S(1)}, u32[]{:S(2)}, u32[]{:S(2)}) collective-permute-start(f32[2,18,1]{1,0,2:T(2,128)S(1)} %get-tuple-element.213), channel_id=1, source_target_pairs={{1,0},{2,1},{3,2},{5,4},{6,5},{7,6},{9,8},{10,9},{11,10},{13,12},{... | collective-permute-start | bytes 440 | tf_op jit(solution)/shard_map/ppermute | solution.py:35
  110.5 6.1 %collective-permute-start.13 = (f32[2,18,1]{1,0,2:T(2,128)S(1)}, f32[2,18,1]{1,0,2:T(2,128)S(1)}, u32[]{:S(2)}, u32[]{:S(2)}) collective-permute-start(f32[2,18,1]{1,0,2:T(2,128)S(1)} %get-tuple-element.212), channel_id=1, source_target_pairs={{0,1},{1,2},{2,3},{4,5},{5,6},{6,7},{8,9},{9,10},{10,11},{12,13},{... | collective-permute-start | bytes 440 | tf_op jit(solution)/shard_map/ppermute | solution.py:32
  166.8 3.0 %collective-permute-start.14 = (f32[2,1,16]{1,0,2:T(2,128)S(1)}, f32[2,1,16]{1,0,2:T(2,128)S(1)}, u32[]{:S(2)}, u32[]{:S(2)}) collective-permute-start(f32[2,1,16]{1,0,2:T(2,128)S(1)} %slice.563), channel_id=1, source_target_pairs={{0,4},{4,8},{8,12},{12,16},{16,20},{20,24},{24,28},{1,5},{5,9},{9,... | collective-permute-start | bytes 392 | tf_op jit(solution)/shard_map/ppermute | solution.py:32
  170.2 3.8 %collective-permute-start.15 = (f32[2,1,16]{1,0,2:T(2,128)S(1)}, f32[2,1,16]{1,0,2:T(2,128)S(1)}, u32[]{:S(2)}, u32[]{:S(2)}) collective-permute-start(f32[2,1,16]{1,0,2:T(2,128)S(1)} %get-tuple-element.217), channel_id=1, source_target_pairs={{4,0},{8,4},{12,8},{16,12},{20,16},{24,20},{28,24},{5,1},{9,5},{13... | collective-permute-start | bytes 392 | tf_op jit(solution)/shard_map/ppermute | solution.py:35
  174.8 6.1 %collective-permute-start.16 = (f32[2,18,1]{1,0,2:T(2,128)S(1)}, f32[2,18,1]{1,0,2:T(2,128)S(1)}, u32[]{:S(2)}, u32[]{:S(2)}) collective-permute-start(f32[2,18,1]{1,0,2:T(2,128)S(1)} %get-tuple-element.211), channel_id=1, source_target_pairs={{1,0},{2,1},{3,2},{5,4},{6,5},{7,6},{9,8},{10,9},{11,10},{13,12},{... | collective-permute-start | bytes 440 | tf_op jit(solution)/shard_map/ppermute | solution.py:35
  176.1 6.1 %collective-permute-start.17 = (f32[2,18,1]{1,0,2:T(2,128)S(1)}, f32[2,18,1]{1,0,2:T(2,128)S(1)}, u32[]{:S(2)}, u32[]{:S(2)}) collective-permute-start(f32[2,18,1]{1,0,2:T(2,128)S(1)} %get-tuple-element.210), channel_id=1, source_target_pairs={{0,1},{1,2},{2,3},{4,5},{5,6},{6,7},{8,9},{9,10},{10,11},{12,13},{... | collective-permute-start | bytes 440 | tf_op jit(solution)/shard_map/ppermute | solution.py:32

commit v2 on v1

--- a/solution.py
+++ b/solution.py
@@ -1,3 +1,5 @@
+import functools
+
 import jax
 import jax.numpy as jnp
 from jax import lax
@@ -10,7 +12,9 @@
 NS = 8
 P_SIZE = 16
 GV = 16
+CELLS = GV * GV
 ITERS = 3
+GAPS = (1, GV, GV + 1, GV - 1)
 
 
 LAMBDA_REG = 0.05
@@ -22,19 +26,6 @@
     length = lax.axis_size(axis)
     pairs = [(i, i + by) for i in range(length) if 0 <= i + by < length]
     return lax.ppermute(x, axis, pairs)
-
-
-def with_halo(block, sides, width):
-    for axis, dim in sides:
-        count = lax.axis_size(axis)
-        forward = [(i, i + 1) for i in range(count - 1)]
-        backward = [(target, source) for source, target in forward]
-        low = lax.ppermute(
-            lax.slice_in_dim(block, block.shape[dim] - width, None, axis=dim), axis, forward
-        )
-        high = lax.ppermute(lax.slice_in_dim(block, 0, width, axis=dim), axis, backward)
-        block = jnp.concatenate([low, block, high], axis=dim)
-    return block
 
 
 def match_kernel(counts, cands, cand_rows, west, north, frames, out, flat, plane, sums):
@@ -124,7 +115,16 @@
             [gathered[0:2] / (REACH * weight_sum), weight_sum / NS], axis=0
         )
         slot = lax.broadcasted_iota(jnp.int32, result.shape, 1)
-        out[seam] = jnp.where(slot < counts[seam], result, 0.0)
+        result = jnp.where(slot < counts[seam], result, 0.0)
+        result = jnp.concatenate([result, jnp.zeros((5, P_SIZE), jnp.float32)], axis=0)
+        source = lax.broadcasted_iota(jnp.int32, (P_SIZE, CELLS + 128), 0)
+        target = lax.broadcasted_iota(jnp.int32, (P_SIZE, CELLS + 128), 1)
+        stride = (GV, 1)[seam]
+        picked = (target == source * stride) | (target == source + CELLS)
+        out[seam] = jnp.dot(
+            result, picked.astype(jnp.float32), precision=PRECISE,
+            preferred_element_type=jnp.float32,
+        )
 
 
 def match_call(counts, cands, west, north, frames):
@@ -134,7 +134,7 @@
     vmem = pl.BlockSpec(memory_space=pltpu.VMEM)
     return pl.pallas_call(
         match_kernel,
-        out_shape=jax.ShapeDtypeStruct((2, 3, P_SIZE), jnp.float32),
+        out_shape=jax.ShapeDtypeStruct((2, 8, CELLS + 128), jnp.float32),
         in_specs=[smem, smem, vmem, vmem, vmem, vmem],
         out_specs=vmem,
         scratch_shapes=[
@@ -145,6 +145,192 @@
         compiler_params=pltpu.CompilerParams(vmem_limit_bytes=40 * 1024 * 1024),
         name="match",
     )(counts, cands, cands, west, north, frames)
+
+
+def mesh_kernel(
+    sizes, scored, springs, matches, shift, back, halo, sent, part, row_parts, col_parts,
+    back_send, back_recv, halo_send, halo_recv, row_send, row_recv, col_send, col_recv,
+):
+    rows, cols = sizes
+    me_row = lax.axis_index("row")
+    me_col = lax.axis_index("col")
+
+    barrier = pltpu.get_barrier_semaphore()
+    for name, count, me in (("row", rows, me_row), ("col", cols, me_col)):
+        for step in range(1, count):
+            pl.semaphore_signal(
+                barrier, inc=1, device_id={name: lax.rem(me + step, count)},
+                device_id_type=pl.DeviceIdType.MESH,
+            )
+    pl.semaphore_wait(barrier, rows + cols - 2)
+
+    has = (me_col < cols - 1, me_row < rows - 1, me_col > 0, me_row > 0)
+    there = ({"col": me_col + 1}, {"row": me_row + 1}, {"col": me_col - 1}, {"row": me_row - 1})
+
+    for side in range(2):
+        @pl.when(jnp.logical_not(has[side]))
+        def _():
+            back[side] = jnp.zeros(back.shape[1:], jnp.float32)
+
+    for side in range(4):
+        @pl.when(jnp.logical_not(has[side]))
+        def _():
+            for turn in range(ITERS):
+                halo[turn, side] = jnp.zeros(halo.shape[2:], jnp.float32)
+
+    def back_copy(seam):
+        return pltpu.make_async_remote_copy(
+            src_ref=scored.at[seam], dst_ref=back.at[seam],
+            send_sem=back_send.at[seam], recv_sem=back_recv.at[seam],
+            device_id=there[seam + 2], device_id_type=pl.DeviceIdType.MESH,
+        )
+
+    for seam in range(2):
+        @pl.when(has[seam + 2])
+        def _():
+            back_copy(seam).start()
+
+    for seam in range(2):
+        @pl.when(has[seam + 2])
+        def _():
+            back_copy(seam).wait_send()
+
+        @pl.when(has[seam])
+        def _():
+            back_copy(seam).wait_recv()
+
+    def halo_copy(turn, side):
+        return pltpu.make_async_remote_copy(
+            src_ref=sent.at[turn], dst_ref=halo.at[turn, (side + 2) % 4],
+            send_sem=halo_send.at[turn, side], recv_sem=halo_recv.at[turn, (side + 2) % 4],
+            device_id=there[side], device_id_type=pl.DeviceIdType.MESH,
+        )
+
+    def row_copy(turn, step):
+        return pltpu.make_async_remote_copy(
+            src_ref=part.at[turn, 0], dst_ref=row_parts.at[turn, step - 1],
+            send_sem=row_send.at[turn, step - 1], recv_sem=row_recv.at[turn, step - 1],
+            device_id={"row": lax.rem(me_row + step, rows)},
+            device_id_type=pl.DeviceIdType.MESH,
+        )
+
+    def col_copy(turn, step):
+        return pltpu.make_async_remote_copy(
+            src_ref=part.at[turn, 1], dst_ref=col_parts.at[turn, step - 1],
+            send_sem=col_send.at[turn, step - 1], recv_sem=col_recv.at[turn, step - 1],
+            device_id={"col": lax.rem(me_col + step, cols)},
+            device_id_type=pl.DeviceIdType.MESH,
+        )
+
+    east = pltpu.roll(back[0, :, :CELLS], GV - 1, 1)
+    south = pltpu.roll(back[1, :, :CELLS], CELLS - GV, 1)
+    west = scored[0, :, :CELLS]
+    north = scored[1, :, :CELLS]
+    for seam in range(2):
+        matches[seam] = back[seam, :3, CELLS : CELLS + P_SIZE]
+    confs = [side[2:3, :] for side in (east, south, west, north)]
+    turns = (GV - 1, CELLS - GV, CELLS - GV + 1, GV)
+    component = lax.broadcasted_iota(jnp.int32, (8, CELLS), 0)
+    forcing = confs[0] * east + confs[1] * south - confs[2] * west - confs[3] * north
+    forcing = jnp.where(component < 2, forcing, 0.0)
+
+    def operate(turn, vector):
+        sent[turn] = vector
+        for side in range(4):
+            @pl.when(has[side])
+            def _():
+                halo_copy(turn, side).start()
+        output = LAMBDA_REG * vector
+        for index, gap in enumerate(GAPS):
+            pull = springs[index : index + 1, :] * (vector - pltpu.roll(vector, CELLS - gap, 1))
+            output = output + pull - pltpu.roll(pull, gap, 1)
+        for side in range(4):
+            @pl.when(has[side])
+            def _():
+                halo_copy(turn, side).wait_send()
+                halo_copy(turn, (side + 2) % 4).wait_recv()
+        for side in range(4):
+            border = pltpu.roll(halo[turn, side], turns[side], 1)
+            output = output + confs[side] * (vector - border)
+        return output
+
+    def lanes(values):
+        folded = values[:, :128] + values[:, 128:]
+        return jnp.sum(folded, axis=0, keepdims=True)
+
+    def two_products(turn, values, applied):
+        total = jnp.concatenate(
+            [lanes(values * values), lanes(values * applied), jnp.zeros((6, 128), jnp.float32)],
+            axis=0,
+        )
+        part[turn, 0] = total
+        for step in range(1, rows):
+            row_copy(turn, step).start()
+        for step in range(1, rows):
+            row_copy(turn, step).wait()
+            total = total + row_parts[turn, step - 1]
+        part[turn, 1] = total
+        for step in range(1, cols):
+            col_copy(turn, step).start()
+        for step in range(1, cols):
+            col_copy(turn, step).wait()
+            total = total + col_parts[turn, step - 1]
+        summed = jnp.sum(total, axis=1, keepdims=True)
+        return summed[0:1], summed[1:2]
+
+    residual = forcing
+    applied = operate(0, residual)
+    norm_now, product = two_products(0, residual, applied)
+    step_length = norm_now / product
+    direction = residual
+    along = applied
+    answer = jnp.zeros_like(forcing)
+    for iteration in range(ITERS):
+        answer = answer + step_length * direction
+        if iteration + 1 < ITERS:
+            residual = residual - step_length * along
+            applied = operate(iteration + 1, residual)
+            norm_next, product = two_products(iteration + 1, residual, applied)
+            beta_ratio = norm_next / norm_now
+            step_length = norm_next / (product - beta_ratio * norm_next / step_length)
+            direction = residual + beta_ratio * direction
+            along = applied + beta_ratio * along
+            norm_now = norm_next
+    shift[...] = answer[:2]
+
+
+def mesh_call(scored, springs):
+    rows = lax.axis_size("row")
+    cols = lax.axis_size("col")
+    vmem = pl.BlockSpec(memory_space=pltpu.VMEM)
+    dma = pltpu.SemaphoreType.DMA
+    return pl.pallas_call(
+        functools.partial(mesh_kernel, (rows, cols)),
+        out_shape=(
+            jax.ShapeDtypeStruct((2, 3, P_SIZE), jnp.float32),
+            jax.ShapeDtypeStruct((2, CELLS), jnp.float32),
+        ),
+        in_specs=[vmem, vmem],
+        out_specs=(vmem, vmem),
+        scratch_shapes=[
+            pltpu.VMEM((2, 8, CELLS + 128), jnp.float32),
+            pltpu.VMEM((ITERS, 4, 8, CELLS), jnp.float32),
+            pltpu.VMEM((ITERS, 8, CELLS), jnp.float32),
+            pltpu.VMEM((ITERS, 2, 8, 128), jnp.float32),
+            pltpu.VMEM((ITERS, rows - 1, 8, 128), jnp.float32),
+            pltpu.VMEM((ITERS, cols - 1, 8, 128), jnp.float32),
+            dma((2,)),
+            dma((2,)),
+            dma((ITERS, 4)),
+            dma((ITERS, 4)),
+            dma((ITERS, rows - 1)),
+            dma((ITERS, rows - 1)),
+            dma((ITERS, cols - 1)),
+            dma((ITERS, cols - 1)),
+        ],
+        compiler_params=pltpu.CompilerParams(collective_id=0, has_side_effects=True),
+        name="mesh",
+    )(scored, springs)
 
 
 def body(patches, windows, candidates, live, edges, stiffness):
@@ -163,80 +349,14 @@
         north_patches,
         windows[0, 0],
     )
-    from_west = scored[0]
-    from_north = scored[1]
-    own_east = shifted(from_west, "col", -1)
-    own_south = shifted(from_north, "row", -1)
-    matches = jnp.stack([own_east, own_south])[None, None]
-    slots = jnp.arange(P_SIZE)
-    picker = (jnp.arange(GV)[None, :] == (slots * GV // P_SIZE)[:, None]).astype(jnp.float32)
-    vertex = jnp.arange(GV * GV)
-    incidence = (edges[0, 0][:, None] == vertex[None, :]).astype(jnp.float32) - (
-        edges[0, 1][:, None] == vertex[None, :]
-    ).astype(jnp.float32)
-    spring = stiffness[0]
-
-    def spread(values):
-        return jnp.dot(values, picker, precision=PRECISE)
-
-    def sample(values):
-        return jnp.dot(values, picker.T, precision=PRECISE)
-
-    conf_east = own_east[2]
-    conf_south = own_south[2]
-    conf_west = from_west[2]
-    conf_north = from_north[2]
-
-    def operate(vector):
-        border = with_halo(vector, (("row", 1), ("col", 2)), 1)
-        flat_field = vector.reshape(2, GV * GV)
-        stretch = jnp.dot(flat_field, incidence.T, precision=PRECISE) * spring
-        output = (LAMBDA_REG * flat_field + jnp.dot(stretch, incidence, precision=PRECISE)).reshape(
-            2, GV, GV
-        )
-        output = output.at[:, :, GV - 1].add(
-            spread(conf_east * sample(vector[:, :, GV - 1] - border[:, 1:-1, -1]))
-        )
-        output = output.at[:, :, 0].add(
-            spread(conf_west * sample(vector[:, :, 0] - border[:, 1:-1, 0]))
-        )
-        output = output.at[:, GV - 1, :].add(
-            spread(conf_south * sample(vector[:, GV - 1, :] - border[:, -1, 1:-1]))
-        )
-        output = output.at[:, 0, :].add(
-            spread(conf_north * sample(vector[:, 0, :] - border[:, 0, 1:-1]))
-        )
-        return output
-
-    forcing = jnp.zeros((2, GV, GV), jnp.float32)
-    forcing = forcing.at[:, :, GV - 1].add(spread(conf_east * own_east[:2]))
-    forcing = forcing.at[:, :, 0].add(-spread(conf_west * from_west[:2]))
-    forcing = forcing.at[:, GV - 1, :].add(spread(conf_south * own_south[:2]))
-    forcing = forcing.at[:, 0, :].add(-spread(conf_north * from_north[:2]))
-    solution = jnp.zeros_like(forcing)
-    residual = forcing
-
-    def two_products(values, applied):
-        return lax.psum((jnp.sum(values * values), jnp.sum(values * applied)), ("row", "col"))
-
-    applied = operate(residual)
-    norm_now, product = two_products(residual, applied)
-    step_length = norm_now / product
-    direction = residual
-    along = applied
-    for iteration in range(ITERS):
-        solution = solution + step_length * direction
-        residual = residual - step_length * along
-        if iteration + 1 < ITERS:
-            applied = operate(residual)
-            norm_next, product = two_products(residual, applied)
-            beta_ratio = norm_next / norm_now
-            step_length = norm_next / (product - beta_ratio * norm_next / step_length)
-            direction = residual + beta_ratio * direction
-            along = applied + beta_ratio * along
-            norm_now = norm_next
-    mesh_shift = solution.reshape(2, GV * GV)[None, None]
-    return (matches, mesh_shift)
+    lower = jnp.minimum(edges[0, 0], edges[0, 1])
+    gap = jnp.abs(edges[0, 0] - edges[0, 1])
+    classes = jnp.array(GAPS + (0,) * 4)
+    spring = jnp.where(gap[None, :] == classes[:, None], stiffness, 0.0)
+    starts = (lower[:, None] == jnp.arange(CELLS)[None, :]).astype(jnp.float32)
+    springs = jnp.dot(spring, starts, precision=PRECISE)
+    matches, mesh_shift = mesh_call(scored, springs)
+    return (matches[None, None], mesh_shift[None, None])
 
 
 def solution(mesh):

time: 233 us -> 75.2 us (0.32)
  blocking collectives: 131 us -> 0 us
  Pallas kernels: 2.86 us -> 46.8 us
  starting transfers between devices: 45.8 us -> 13.5 us
  waiting for transfers between devices: 11.9 us -> 1.71 us
  between operations: 12.2 us -> 2.01 us
  matrix products: 9.83 us -> 1.65 us
  local copies, waits for them, and re-layouts: 15 us -> 7.64 us
    psum x3 -> x0, blocking collectives: 131 us -> none  [two_products(): lax.psum((jnp.sum(values * values), jnp.sum(values * applied)), ('row', '...]
    pallas_call x1 -> x2, Pallas kernels: 2.86 us -> 46.8 us  [the longest x1 43.7 us: mesh_call(): pl.pallas_call(functools.partial(mesh_kernel, (rows, cols)), out_shape=(j...]
    ppermute x12 -> x0, starting transfers between devices: 29.7 us -> none  [the longest x6 22 us: with_halo(): lax.ppermute(lax.slice_in_dim(block, block.shape[dim] - width, None, axis...]
    ppermute x12 -> x0, waiting for transfers between devices: 9.48 us -> none  [the longest x6 6.58 us: with_halo(): lax.ppermute(lax.slice_in_dim(block, 0, width, axis=dim), axis, backward)]
    dot_general x34 -> x1, matrix products: 9.83 us -> 1.65 us  [body(): springs = jnp.dot(spring, starts, precision=PRECISE)]
    scatter-add x10 -> x0, local copies, waits for them, and re-layouts: 5.5 us -> none  [the longest x3 3.65 us: operate(): output.at[:, GV - 1, :]]
    ppermute x6 -> x4, starting transfers between devices: 16.1 us -> 13.5 us  [shifted(): return lax.ppermute(x, axis, pairs)]
  transfers between devices with their start and end apart: 18 -> 4, of which waited for: 9 -> 1; matrix products, arithmetic and copies ran while one was open for 5% -> 9% of each run, Pallas kernels for 0% -> 0%
where the time goes in v2:
time: 75.2 us; the launch traced here: 75 us
  Pallas kernels  46.8 us (62%)
  starting transfers between devices  13.5 us (18%)
  local copies, waits for them, and re-layouts  7.64 us (10%)
  between operations  2.01 us (3%)
  waiting for transfers between devices  1.71 us (2%)
  matrix products  1.65 us (2%)
  other arithmetic  1.57 us (2%)
    pallas_call x1, Pallas kernels, mesh_call(): pl.pallas_call(functools.partial(mesh_kernel, (rows, cols)), out_shape=(j...  43.7 us
    ppermute x4, starting transfers between devices, shifted(): return lax.ppermute(x, axis, pairs)  13.5 us
    pallas_call x1, Pallas kernels, match_call(): pl.pallas_call(match_kernel, out_shape=jax.ShapeDtypeStruct((2, 8, CELLS...  3.18 us
    squeeze x1, local copies, waits for them, and re-layouts, body(): north_patches = shifted(patches[0, 0, 1], 'row', 1)  2.29 us
    unnamed x5, local copies, waits for them, and re-layouts  1.9 us
    ppermute x4, waiting for transfers between devices, shifted(): return lax.ppermute(x, axis, pairs)  1.71 us
    dot_general x1, matrix products, body(): springs = jnp.dot(spring, starts, precision=PRECISE)  1.65 us
  transfers between devices with their start and end apart: 4, of which 1 were waited for; matrix products, arithmetic and copies ran while one was open for 9% of the time, Pallas kernels for 0%

profile of v2, /device:TPU:0, one launch (start us, length us, event | category | flops | bytes accessed | tf_op | source)
XLA Modules:
  0.0 75.0 jit_solution(1122504768760003428)
XLA Ops:
  0.6 0.0 copy-start
  0.6 0.8 %slice_bitcast_fusion.3 = (s32[2,128]{1,0:T(2,128)S(1)}, s32[2,128]{1,0:T(2,128)S(1)}) fusion(s32[1,1,2,2,128]{4,3,2,1,0:T(2,128)} %param.9), kind=kLoop, calls=%fused_computation.16 | loop fusion | bytes 4096 | tf_op jit(solution)/shard_map/squeeze | solution.py:341
  1.5 4.9 %collective-permute-start = (s32[2,128]{1,0:T(2,128)S(1)}, s32[2,128]{1,0:T(2,128)S(1)}, u32[]{:S(2)}, u32[]{:S(2)}) collective-permute-start(s32[2,128]{1,0:T(2,128)S(1)} %get-tuple-element.12), channel_id=1, source_target_pairs={{0,1},{1,2},{2,3},{4,5},{5,6},{6,7},{8,9},{9,10},{10,11},{12,13},{... | collective-permute-start | bytes 3080 | tf_op jit(solution)/shard_map/ppermute | solution.py:28
  6.4 1.5 %collective-permute-start.1 = (s32[2,128]{1,0:T(2,128)S(1)}, s32[2,128]{1,0:T(2,128)S(1)}, u32[]{:S(2)}, u32[]{:S(2)}) collective-permute-start(s32[2,128]{1,0:T(2,128)S(1)} %get-tuple-element.13), channel_id=1, source_target_pairs={{0,4},{4,8},{8,12},{12,16},{16,20},{20,24},{24,28},{1,5},{5,9},{9,... | collective-permute-start | bytes 3080 | tf_op jit(solution)/shard_map/ppermute | solution.py:28
  7.8 2.3 %slice_bitcast_fusion = (bf16[16,128,128]{2,1,0:T(8,128)(2,1)}, bf16[16,128,128]{2,1,0:T(8,128)(2,1)}) fusion(bf16[1,1,2,16,128,128]{5,4,3,2,1,0:T(8,128)(2,1)} %param.7), kind=kLoop, calls=%fused_computation.2 | loop fusion | bytes 2097152 | tf_op jit(solution)/shard_map/squeeze | solution.py:340
  10.1 3.4 %collective-permute-start.2 = (bf16[16,128,128]{2,1,0:T(8,128)(2,1)}, bf16[16,128,128]{2,1,0:T(8,128)(2,1)S(1)}, u32[]{:S(2)}, u32[]{:S(2)}) collective-permute-start(bf16[16,128,128]{2,1,0:T(8,128)(2,1)} %get-tuple-element.9), channel_id=1, source_target_pairs={{0,1},{1,2},{2,3},{4,5},{5,6},{6,7},{8,9},{9,10},{10,11},{12,13},{... | collective-permute-start | bytes 1572872 | tf_op jit(solution)/shard_map/ppermute | solution.py:28
  13.5 3.8 %collective-permute-start.3 = (bf16[16,128,128]{2,1,0:T(8,128)(2,1)}, bf16[16,128,128]{2,1,0:T(8,128)(2,1)S(1)}, u32[]{:S(2)}, u32[]{:S(2)}) collective-permute-start(bf16[16,128,128]{2,1,0:T(8,128)(2,1)} %get-tuple-element.8), channel_id=1, source_target_pairs={{0,4},{4,8},{8,12},{12,16},{16,20},{20,24},{24,28},{1,5},{5,9},{9,... | collective-permute-start | bytes 1572872 | tf_op jit(solution)/shard_map/ppermute | solution.py:28
  17.4 1.3 %constant_dynamic-slice_fusion.1 = (s32[1,1,1]{0,2,1:T(1,128)}, s32[1,1,1]{0,2,1:T(1,128)}) fusion(s32[8,4,2]{0,2,1:T(2,128)} %param.10, s32[]{:T(128)S(6)} %select_n.19, s32[]{:T(128)S(6)} %max.6, s32[]{:T(128)S(6)} %max.7, s32[]{:T(128)S(6)} %select_n.21), kind=kLoop, calls=%fused_computation.19 | loop fusion | bytes 32 | tf_op jit(solution)/shard_map/dynamic_slice | solution.py:343
  20.0 0.7 reduce.1
  20.7 0.8 %abs_reduce_fusion = (s32[705]{0:T(1024)S(1)}, s32[705]{0:T(1024)S(1)}) fusion(s32[1,2,705]{2,1,0:T(2,128)} %param.11), kind=kLoop, calls=%fused_computation.13 | loop fusion | flops 2115 | bytes 11280 | tf_op jit(solution)/shard_map/abs | solution.py:353
  21.5 1.7 %fusion.springs = f32[8,256]{1,0:T(8,128)} fusion(s32[705]{0:T(1024)S(1)} %get-tuple-element.7, f32[705]{0:T(1024)S(1)} %reduce.1, s32[705]{0:T(1024)S(1)} %get-tuple-element.6, s32[8]{0:T(128)} %constant.26.clone), kind=kOutput, calls=%fused_computation.1 | convolution fusion | flops 17517840 | bytes 16684 | tf_op jit(solution)/shard_map/dot_general | solution.py:357
  23.2 0.1 pad_add_fusion.1.counts
  23.2 0.0 collective-permute-done
  23.2 0.0 collective-permute-done.1
  23.2 1.7 %collective-permute-done.2.west = bf16[16,128,128]{2,1,0:T(8,128)(2,1)S(1)} collective-permute-done((bf16[16,128,128]{2,1,0:T(8,128)(2,1)}, bf16[16,128,128]{2,1,0:T(8,128)(2,1)S(1)}, u32[]{:S(2)}, u32[]{:S(2)}) %collective-permute-start.2) | collective-permute-done | bytes 524320 | tf_op jit(solution)/shard_map/ppermute | solution.py:28
  24.9 0.0 collective-permute-done.3.north
  24.9 0.0 copy-done
  25.0 3.2 %match.1.scored = f32[2,8,384]{2,1,0:T(8,128)S(1)} custom-call(s32[2]{0:T(128)S(1)} %pad_add_fusion.1.counts, s32[2,2,128]{2,1,0:T(2,128)S(1)} %pad_add_fusion.cands.cand_rows, s32[2,2,128]{2,1,0:T(2,128)S(1)} %pad_add_fusion.cands.cand_rows, bf16[16,128,128]{2,1,0:T(8,128)(2,1)S(1)} %collective-permute-done.2.west, ...), custom_call_target="tpu_custom_call" | custom-call | tf_op jit(solution)/shard_map/match/pallas_call | solution.py:135
  28.1 0.0 copy-start.1
  28.1 0.6 copy-done.1
  28.8 43.7 %mesh.1 = (f32[2,3,16]{2,1,0:T(4,128)}, f32[2,256]{1,0:T(2,128)}) custom-call(f32[2,8,384]{2,1,0:T(8,128)} %copy-done.1, f32[8,256]{1,0:T(8,128)} %fusion.springs), custom_call_target="tpu_custom_call" | custom-call | tf_op jit(solution)/shard_map/mesh/pallas_call | solution.py:307
  72.4 1.3 %copy.11 = f32[2,3,16]{2,0,1:T(2,128)} copy(f32[2,3,16]{2,1,0:T(4,128)} %get-tuple-element.4) | data formatting | bytes 768 | tf_op jit(solution)/shard_map/mesh/pallas_call | solution.py:307
  73.7 1.3 %copy.13 = f32[1,1,2,256]{3,2,1,0:T(2,128)} copy(f32[1,1,2,256]{3,2,1,0:T(2,128)} %bitcast.21) | data formatting | bytes 4096
  (1 shorter events, 0.0 us)
Async XLA Ops:
  0.6 24.3 %copy-start = (bf16[1,1,2,16,36864]{4,3,2,1,0:T(8,128)(2,1)S(1)}, bf16[1,1,2,16,36864]{4,3,2,1,0:T(8,128)(2,1)}, u32[]{:S(2)}) copy-start(bf16[1,1,2,16,36864]{4,3,2,1,0:T(8,128)(2,1)} %param.8) | copy-start | bytes 7077892
  1.5 21.7 %collective-permute-start = (s32[2,128]{1,0:T(2,128)S(1)}, s32[2,128]{1,0:T(2,128)S(1)}, u32[]{:S(2)}, u32[]{:S(2)}) collective-permute-start(s32[2,128]{1,0:T(2,128)S(1)} %get-tuple-element.12), channel_id=1, source_target_pairs={{0,1},{1,2},{2,3},{4,5},{5,6},{6,7},{8,9},{9,10},{10,11},{12,13},{... | collective-permute-start | bytes 3080 | tf_op jit(solution)/shard_map/ppermute | solution.py:28
  6.4 16.9 %collective-permute-start.1 = (s32[2,128]{1,0:T(2,128)S(1)}, s32[2,128]{1,0:T(2,128)S(1)}, u32[]{:S(2)}, u32[]{:S(2)}) collective-permute-start(s32[2,128]{1,0:T(2,128)S(1)} %get-tuple-element.13), channel_id=1, source_target_pairs={{0,4},{4,8},{8,12},{12,16},{16,20},{20,24},{24,28},{1,5},{5,9},{9,... | collective-permute-start | bytes 3080 | tf_op jit(solution)/shard_map/ppermute | solution.py:28
  10.1 14.8 %collective-permute-start.2 = (bf16[16,128,128]{2,1,0:T(8,128)(2,1)}, bf16[16,128,128]{2,1,0:T(8,128)(2,1)S(1)}, u32[]{:S(2)}, u32[]{:S(2)}) collective-permute-start(bf16[16,128,128]{2,1,0:T(8,128)(2,1)} %get-tuple-element.9), channel_id=1, source_target_pairs={{0,1},{1,2},{2,3},{4,5},{5,6},{6,7},{8,9},{9,10},{10,11},{12,13},{... | collective-permute-start | bytes 1572872 | tf_op jit(solution)/shard_map/ppermute | solution.py:28
  13.5 11.4 %collective-permute-start.3 = (bf16[16,128,128]{2,1,0:T(8,128)(2,1)}, bf16[16,128,128]{2,1,0:T(8,128)(2,1)S(1)}, u32[]{:S(2)}, u32[]{:S(2)}) collective-permute-start(bf16[16,128,128]{2,1,0:T(8,128)(2,1)} %get-tuple-element.8), channel_id=1, source_target_pairs={{0,4},{4,8},{8,12},{12,16},{16,20},{20,24},{24,28},{1,5},{5,9},{9,... | collective-permute-start | bytes 1572872 | tf_op jit(solution)/shard_map/ppermute | solution.py:28
  28.1 0.6 copy-start.1

commit v3 on v2

--- a/solution.py
+++ b/solution.py
@@ -18,18 +18,85 @@
 
 
 LAMBDA_REG = 0.05
+CENTER = 8.0
+SPAN = 8.0
 EPSILON = 1e-05
 PRECISE = lax.Precision.HIGHEST
 
 
-def shifted(x, axis, by):
-    length = lax.axis_size(axis)
-    pairs = [(i, i + by) for i in range(length) if 0 <= i + by < length]
-    return lax.ppermute(x, axis, pairs)
-
-
-def match_kernel(counts, cands, cand_rows, west, north, frames, out, flat, plane, sums):
-    patch_size = west.shape[-1]
+def pass_kernel(sizes, patches, cands, patches_out, cands_out, send, recv):
+    rows, cols = sizes
+    me_row = lax.axis_index("row")
+    me_col = lax.axis_index("col")
+    gives = (me_col < cols - 1, me_row < rows - 1)
+    takes = (me_col > 0, me_row > 0)
+    ahead = ({"col": me_col + 1}, {"row": me_row + 1})
+    behind = ({"col": me_col - 1}, {"row": me_row - 1})
+    barrier = pltpu.get_barrier_semaphore()
+    for flags, where in ((gives, ahead), (takes, behind)):
+        for seam in range(2):
+            @pl.when(flags[seam])
+            def _():
+                pl.semaphore_signal(
+                    barrier, inc=1, device_id=where[seam], device_id_type=pl.DeviceIdType.MESH
+                )
+    pl.semaphore_wait(barrier, sum(flag.astype(jnp.int32) for flag in gives + takes))
+
+    def copies(seam):
+        return [
+            pltpu.make_async_remote_copy(
+                src_ref=source.at[seam], dst_ref=target.at[seam],
+                send_sem=send.at[seam, which], recv_sem=recv.at[seam, which],
+                device_id=ahead[seam], device_id_type=pl.DeviceIdType.MESH,
+            )
+            for which, (source, target) in enumerate(
+                ((cands, cands_out), (patches, patches_out))
+            )
+        ]
+
+    for seam in range(2):
+        @pl.when(gives[seam])
+        def _():
+            for copy in copies(seam):
+                copy.start()
+
+    for seam in range(2):
+        @pl.when(gives[seam])
+        def _():
+            for copy in copies(seam):
+                copy.wait_send()
+
+        @pl.when(takes[seam])
+        def _():
+            for copy in copies(seam):
+                copy.wait_recv()
+
+
+def pass_call(patches, cands):
+    anywhere = pl.BlockSpec(memory_space=pl.ANY)
+    dma = pltpu.SemaphoreType.DMA
+    return pl.pallas_call(
+        functools.partial(pass_kernel, (lax.axis_size("row"), lax.axis_size("col"))),
+        out_shape=(
+            jax.ShapeDtypeStruct(patches.shape, patches.dtype),
+            jax.ShapeDtypeStruct(cands.shape, cands.dtype),
+        ),
+        in_specs=[anywhere, anywhere],
+        out_specs=(anywhere, anywhere),
+        scratch_shapes=[dma((2, 2)), dma((2, 2))],
+        compiler_params=pltpu.CompilerParams(collective_id=1, has_side_effects=True),
+        name="hand_over",
+    )(patches, cands)
+
+
+def match_kernel(live, cands, cand_rows, patches, frames, out, flat, plane, sums):
+    me_row = lax.axis_index("row")
+    me_col = lax.axis_index("col")
+    counts = (
+        jnp.where(me_col > 0, live[me_row, jnp.maximum(me_col - 1, 0), 0], 0),
+        jnp.where(me_row > 0, live[jnp.maximum(me_row - 1, 0), me_col, 1], 0),
+    )
+    patch_size = patches.shape[-1]
     chunks = frames.shape[-1] // 128
     pitch = chunks + 1
     half = patch_size // 2
@@ -40,8 +107,6 @@
         return jnp.sum(values.reshape(half // 8, 8, 128), axis=0)
 
     for seam in range(2):
-        patches = (west, north)[seam]
-
         def spread_chunk(chunk, carry):
             start = pl.multiple_of(chunk * 128, 128)
             piece = frames[seam, :, pl.ds(start, 128)].astype(jnp.float32)
@@ -51,7 +116,7 @@
         lax.fori_loop(0, chunks, spread_chunk, 0, unroll=8)
 
         def one_patch(slot, carry):
-            plane[...] = patches[slot].astype(jnp.float32)
+            plane[...] = patches[seam, slot].astype(jnp.float32)
             parts = [plane[pl.ds(parity, half, stride=2), :] for parity in range(2)]
             own_sum = fold(parts[0] + parts[1])
             own_square = fold(parts[0] * parts[0] + parts[1] * parts[1])
@@ -127,15 +192,15 @@
         )
 
 
-def match_call(counts, cands, west, north, frames):
-    patch_size = west.shape[-1]
+def match_call(live, cands, patches, frames):
+    patch_size = patches.shape[-1]
     pitch = frames.shape[-1] // 128 + 1
     smem = pl.BlockSpec(memory_space=pltpu.SMEM)
     vmem = pl.BlockSpec(memory_space=pltpu.VMEM)
     return pl.pallas_call(
         match_kernel,
         out_shape=jax.ShapeDtypeStruct((2, 8, CELLS + 128), jnp.float32),
-        in_specs=[smem, smem, vmem, vmem, vmem, vmem],
+        in_specs=[smem, smem, vmem, vmem, vmem],
         out_specs=vmem,
         scratch_shapes=[
             pltpu.VMEM((P_SIZE * pitch, 128), jnp.float32),
@@ -144,7 +209,7 @@
         ],
         compiler_params=pltpu.CompilerParams(vmem_limit_bytes=40 * 1024 * 1024),
         name="match",
-    )(counts, cands, cands, west, north, frames)
+    )(live, cands, cands, patches, frames)
 
 
 def mesh_kernel(
@@ -206,18 +271,18 @@
             device_id=there[side], device_id_type=pl.DeviceIdType.MESH,
         )
 
-    def row_copy(turn, step):
+    def row_copy(step):
         return pltpu.make_async_remote_copy(
-            src_ref=part.at[turn, 0], dst_ref=row_parts.at[turn, step - 1],
-            send_sem=row_send.at[turn, step - 1], recv_sem=row_recv.at[turn, step - 1],
+            src_ref=part.at[0], dst_ref=row_parts.at[step - 1],
+            send_sem=row_send.at[step - 1], recv_sem=row_recv.at[step - 1],
             device_id={"row": lax.rem(me_row + step, rows)},
             device_id_type=pl.DeviceIdType.MESH,
         )
 
-    def col_copy(turn, step):
+    def col_copy(step):
         return pltpu.make_async_remote_copy(
-            src_ref=part.at[turn, 1], dst_ref=col_parts.at[turn, step - 1],
-            send_sem=col_send.at[turn, step - 1], recv_sem=col_recv.at[turn, step - 1],
+            src_ref=part.at[1], dst_ref=col_parts.at[step - 1],
+            send_sem=col_send.at[step - 1], recv_sem=col_recv.at[step - 1],
             device_id={"col": lax.rem(me_col + step, cols)},
             device_id_type=pl.DeviceIdType.MESH,
         )
@@ -258,44 +323,60 @@
         folded = values[:, :128] + values[:, 128:]
         return jnp.sum(folded, axis=0, keepdims=True)
 
-    def two_products(turn, values, applied):
-        total = jnp.concatenate(
-            [lanes(values * values), lanes(values * applied), jnp.zeros((6, 128), jnp.float32)],
-            axis=0,
-        )
-        part[turn, 0] = total
-        for step in range(1, rows):
-            row_copy(turn, step).start()
-        for step in range(1, rows):
-            row_copy(turn, step).wait()
-            total = total + row_parts[turn, step - 1]
-        part[turn, 1] = total
-        for step in range(1, cols):
-            col_copy(turn, step).start()
-        for step in range(1, cols):
-            col_copy(turn, step).wait()
-            total = total + col_parts[turn, step - 1]
-        summed = jnp.sum(total, axis=1, keepdims=True)
-        return summed[0:1], summed[1:2]
-
-    residual = forcing
-    applied = operate(0, residual)
-    norm_now, product = two_products(0, residual, applied)
-    step_length = norm_now / product
-    direction = residual
-    along = applied
-    answer = jnp.zeros_like(forcing)
+    basis = [forcing]
+    for turn in range(ITERS):
+        image = operate(turn, basis[-1])
+        basis.append((image - CENTER * basis[-1]) * (1.0 / SPAN))
+
+    pairs = [lanes(basis[(n + 0) // 2] * basis[(n + 1) // 2]) for n in range(2 * ITERS)]
+    pad = part.shape[1] - len(pairs)
+    total = jnp.concatenate(pairs + [jnp.zeros((pad, 128), jnp.float32)], axis=0)
+    part[0] = total
+    for step in range(1, rows):
+        row_copy(step).start()
+    for step in range(1, rows):
+        row_copy(step).wait()
+        total = total + row_parts[step - 1]
+    part[1] = total
+    for step in range(1, cols):
+        col_copy(step).start()
+    for step in range(1, cols):
+        col_copy(step).wait()
+        total = total + col_parts[step - 1]
+    summed = jnp.sum(total, axis=1, keepdims=True)
+    moments = [summed[n : n + 1] for n in range(2 * ITERS)]
+
+    def inner(left, right):
+        return sum(
+            x * y * moments[i + j] for i, x in enumerate(left) for j, y in enumerate(right)
+        )
+
+    def apply(terms):
+        kept = [CENTER * term for term in terms]
+        raised = [SPAN * term for term in terms]
+        middle = [low + high for low, high in zip(kept[1:], raised[:-1])]
+        return kept[:1] + middle + raised[-1:]
+
+    def combine(left, scale, right):
+        joined = [x + scale * y for x, y in zip(left, right)]
+        longer = left if len(left) > len(right) else [scale * y for y in right]
+        return joined + longer[len(joined) :]
+
+    one = jnp.ones((1, 1), jnp.float32)
+    residual = [one]
+    direction = [one]
+    answer = []
+    norm_now = moments[0]
     for iteration in range(ITERS):
-        answer = answer + step_length * direction
+        image = apply(direction)
+        step_length = norm_now / inner(direction, image)
+        answer = combine(answer, step_length, direction)
         if iteration + 1 < ITERS:
-            residual = residual - step_length * along
-            applied = operate(iteration + 1, residual)
-            norm_next, product = two_products(iteration + 1, residual, applied)
-            beta_ratio = norm_next / norm_now
-            step_length = norm_next / (product - beta_ratio * norm_next / step_length)
-            direction = residual + beta_ratio * direction
-            along = applied + beta_ratio * along
+            residual = combine(residual, -step_length, image)
+            norm_next = inner(residual, residual)
+            direction = combine(residual, norm_next / norm_now, direction)
             norm_now = norm_next
+    answer = sum(scale * vector for scale, vector in zip(answer, basis))
     shift[...] = answer[:2]
 
 
@@ -316,17 +397,17 @@
             pltpu.VMEM((2, 8, CELLS + 128), jnp.float32),
             pltpu.VMEM((ITERS, 4, 8, CELLS), jnp.float32),
             pltpu.VMEM((ITERS, 8, CELLS), jnp.float32),
-            pltpu.VMEM((ITERS, 2, 8, 128), jnp.float32),
-            pltpu.VMEM((ITERS, rows - 1, 8, 128), jnp.float32),
-            pltpu.VMEM((ITERS, cols - 1, 8, 128), jnp.float32),
+            pltpu.VMEM((2, 8, 128), jnp.float32),
+            pltpu.VMEM((rows - 1, 8, 128), jnp.float32),
+            pltpu.VMEM((cols - 1, 8, 128), jnp.float32),
             dma((2,)),
             dma((2,)),
             dma((ITERS, 4)),
             dma((ITERS, 4)),
-            dma((ITERS, rows - 1)),
-            dma((ITERS, rows - 1)),
-            dma((ITERS, cols - 1)),
-            dma((ITERS, cols - 1)),
+            dma((rows - 1,)),
+            dma((rows - 1,)),
+            dma((cols - 1,)),
+            dma((cols - 1,)),
         ],
         compiler_params=pltpu.CompilerParams(collective_id=0, has_side_effects=True),
         name="mesh",
@@ -334,21 +415,8 @@
 
 
 def body(patches, windows, candidates, live, edges, stiffness):
-    tile_row = lax.axis_index("row")
-    tile_col = lax.axis_index("col")
-    west_patches = shifted(patches[0, 0, 0], "col", 1)
-    north_patches = shifted(patches[0, 0, 1], "row", 1)
-    west_cands = shifted(candidates[0, 0, 0], "col", 1)
-    north_cands = shifted(candidates[0, 0, 1], "row", 1)
-    count_west = jnp.where(tile_col > 0, live[tile_row, jnp.maximum(tile_col - 1, 0), 0], 0)
-    count_north = jnp.where(tile_row > 0, live[jnp.maximum(tile_row - 1, 0), tile_col, 1], 0)
-    scored = match_call(
-        jnp.stack([count_west, count_north]),
-        jnp.stack([west_cands, north_cands]),
-        west_patches,
-        north_patches,
-        windows[0, 0],
-    )
+    given, cands = pass_call(patches[0, 0], candidates[0, 0])
+    scored = match_call(live, cands, given, windows[0, 0])
     lower = jnp.minimum(edges[0, 0], edges[0, 1])
     gap = jnp.abs(edges[0, 0] - edges[0, 1])
     classes = jnp.array(GAPS + (0,) * 4)

time: 75.2 us -> 57.9 us (0.77)
  starting transfers between devices: 13.5 us -> 0 us
  Pallas kernels: 46.8 us -> 48.6 us
  waiting for transfers between devices: 1.71 us -> 0 us
  other arithmetic: 1.57 us -> 0.04 us
  between operations: 2.01 us -> 0.7 us
    pallas_call x0 -> x1, Pallas kernels: none -> 15.3 us  [pass_call(): pl.pallas_call(functools.partial(pass_kernel, (lax.axis_size('row'), lax....]
    pallas_call x1, Pallas kernels: 43.7 us -> 29.9 us  [mesh_call(): pl.pallas_call(functools.partial(mesh_kernel, (rows, cols)), out_shape=(j...]
    ppermute x4 -> x0, starting transfers between devices: 13.5 us -> none  [shifted(): return lax.ppermute(x, axis, pairs)]
    unnamed x5 -> x16, local copies, waits for them, and re-layouts: 1.9 us -> 6.23 us
    squeeze x2 -> x0, local copies, waits for them, and re-layouts: 3.14 us -> none  [the longest x1 2.29 us: body(): north_patches = shifted(patches[0, 0, 1], 'row', 1)]
    ppermute x4 -> x0, waiting for transfers between devices: 1.71 us -> none  [shifted(): return lax.ppermute(x, axis, pairs)]
    dynamic_slice x1 -> x0, local copies, waits for them, and re-layouts: 1.35 us -> none  [body(): live[tile_row, jnp.maximum(tile_col - 1, 0), 0]]
    abs x1, other arithmetic: 0.79 us -> 0.03 us  [body(): gap = jnp.abs(edges[0, 0] - edges[0, 1])]
  transfers between devices with their start and end apart: 4 -> 0, of which waited for: 1 -> 0; matrix products, arithmetic and copies ran while one was open for 9% -> 0% of each run, Pallas kernels for 0% -> 0%
where the time goes in v3:
time: 57.9 us
  Pallas kernels  48.6 us (84%)
  local copies, waits for them, and re-layouts  7.49 us (13%)
  matrix products  0.99 us (2%)
  between operations  0.7 us (1%)
    pallas_call x1, Pallas kernels, mesh_call(): pl.pallas_call(functools.partial(mesh_kernel, (rows, cols)), out_shape=(j...  29.9 us
    pallas_call x1, Pallas kernels, pass_call(): pl.pallas_call(functools.partial(pass_kernel, (lax.axis_size('row'), lax....  15.3 us
    unnamed x16, local copies, waits for them, and re-layouts  6.23 us
    pallas_call x1, Pallas kernels, match_call(): pl.pallas_call(match_kernel, out_shape=jax.ShapeDtypeStruct((2, 8, CELLS...  3.45 us
    pallas_call x1, local copies, waits for them, and re-layouts, mesh_call(): pl.pallas_call(functools.partial(mesh_kernel, (rows, cols)), out_shape=(j...  1.26 us

profile of v3, /device:TPU:0, one launch (start us, length us, event | category | flops | bytes accessed | tf_op | source)
XLA Modules:
  0.0 57.9 jit_solution(7347315436603398202)
XLA Ops:
  0.6 0.0 copy-start.6
  0.6 0.0 copy-start.4
  0.7 0.0 copy-start.5
  0.7 15.3 %hand_over.1 = (bf16[2,16,128,128]{3,2,1,0:T(8,128)(2,1)}, s32[2,2,128]{2,1,0:T(2,128)}) custom-call(bf16[2,16,128,128]{3,2,1,0:T(8,128)(2,1)} %bitcast.8, s32[2,2,128]{2,1,0:T(2,128)} %bitcast.10), custom_call_target="tpu_custom_call" | custom-call | tf_op jit(solution)/shard_map/hand_over/pallas_call | solution.py:78
  15.9 0.8 %copy.9.live = s32[8,4,2]{2,1,0:T(4,128)S(1)} copy(s32[8,4,2]{0,2,1:T(2,128)} %param.10) | data formatting | bytes 512 | tf_op args[3]
  16.7 0.0 copy-start
  16.7 1.7 %copy-done = bf16[1,1,2,16,36864]{4,3,2,1,0:T(8,128)(2,1)S(1)} copy-done((bf16[1,1,2,16,36864]{4,3,2,1,0:T(8,128)(2,1)S(1)}, bf16[1,1,2,16,36864]{4,3,2,1,0:T(8,128)(2,1)}, u32[]{:S(2)}) %copy-start) | copy-done | bytes 2359320
  18.4 0.0 copy-start.1
  18.4 1.2 %copy-done.1 = bf16[2,16,128,128]{3,2,1,0:T(8,128)(2,1)S(1)} copy-done((bf16[2,16,128,128]{3,2,1,0:T(8,128)(2,1)S(1)}, bf16[2,16,128,128]{3,2,1,0:T(8,128)(2,1)}, u32[]{:S(2)}) %copy-start.1) | copy-done | bytes 1048600
  19.6 0.0 copy-start.3
  19.6 0.7 %copy-done.3 = s32[2,2,128]{2,1,0:T(2,128)S(1)} copy-done((s32[2,2,128]{2,1,0:T(2,128)S(1)}, s32[2,2,128]{2,1,0:T(2,128)}, u32[]{:S(2)}) %copy-start.3) | copy-done | bytes 2072
  20.3 3.5 %match.1.scored = f32[2,8,384]{2,1,0:T(8,128)S(1)} custom-call(s32[8,4,2]{2,1,0:T(4,128)S(1)} %copy.9.live, s32[2,2,128]{2,1,0:T(2,128)S(1)} %copy-done.3, s32[2,2,128]{2,1,0:T(2,128)S(1)} %copy-done.3, bf16[2,16,128,128]{3,2,1,0:T(8,128)(2,1)S(1)} %copy-done.1, bf16[2,16,36864]{2,1,0:T(8,128)(2,1)S(1)} %bitcast.7), custom_call_target="tpu_custom_call" | custom-call | tf_op jit(solution)/shard_map/match/pallas_call | solution.py:200
  23.7 0.0 copy-start.2
  23.7 0.6 %copy-done.2 = f32[2,8,384]{2,1,0:T(8,128)} copy-done((f32[2,8,384]{2,1,0:T(8,128)}, f32[2,8,384]{2,1,0:T(8,128)S(1)}, u32[]{:S(2)}) %copy-start.2) | copy-done | bytes 24600
  24.3 0.0 copy-done.4
  24.4 0.0 copy-done.5
  24.4 0.0 copy-done.6
  24.4 1.0 %fusion.springs = f32[8,256]{1,0:T(8,128)} fusion(s32[705]{0:T(1024)S(1)} %get-tuple-element.11, f32[705]{0:T(1024)S(1)} %reduce.1, s32[705]{0:T(1024)S(1)} %get-tuple-element.10, s32[8]{0:T(128)S(1)} %copy-done.6), kind=kOutput, calls=%fused_computation.1 | convolution fusion | flops 17517840 | bytes 16684 | tf_op jit(solution)/shard_map/dot_general | solution.py:425
  25.4 29.9 %mesh.1 = (f32[2,3,16]{2,1,0:T(4,128)}, f32[2,256]{1,0:T(2,128)}) custom-call(f32[2,8,384]{2,1,0:T(8,128)} %copy-done.2, f32[8,256]{1,0:T(8,128)} %fusion.springs), custom_call_target="tpu_custom_call" | custom-call | tf_op jit(solution)/shard_map/mesh/pallas_call | solution.py:388
  55.4 1.3 %copy.12 = f32[2,3,16]{2,0,1:T(2,128)} copy(f32[2,3,16]{2,1,0:T(4,128)} %get-tuple-element.8) | data formatting | bytes 768 | tf_op jit(solution)/shard_map/mesh/pallas_call | solution.py:388
  56.6 1.3 %copy.14 = f32[1,1,2,256]{3,2,1,0:T(2,128)} copy(f32[1,1,2,256]{3,2,1,0:T(2,128)} %bitcast.11) | data formatting | bytes 4096
  (2 shorter events, 0.0 us)
Async XLA Ops:
  0.6 23.8 %copy-start.6 = (s32[8]{0:T(128)S(1)}, s32[8]{0:T(128)}, u32[]{:S(2)}) copy-start(s32[8]{0:T(128)} %constant.4.clone) | copy-start | bytes 100
  0.6 23.7 %copy-start.4 = (s32[1,2,705]{2,1,0:T(2,128)S(1)}, s32[1,2,705]{2,1,0:T(2,128)}, u32[]{:S(2)}) copy-start(s32[1,2,705]{2,1,0:T(2,128)} %param.11) | copy-start | bytes 16924
  0.7 23.7 %copy-start.5 = (f32[1,705]{1,0:T(1,128)S(1)}, f32[1,705]{1,0:T(1,128)}, u32[]{:S(2)}) copy-start(f32[1,705]{1,0:T(1,128)} %param.12) | copy-start | bytes 8464
  16.7 1.7 %copy-start = (bf16[1,1,2,16,36864]{4,3,2,1,0:T(8,128)(2,1)S(1)}, bf16[1,1,2,16,36864]{4,3,2,1,0:T(8,128)(2,1)}, u32[]{:S(2)}) copy-start(bf16[1,1,2,16,36864]{4,3,2,1,0:T(8,128)(2,1)} %param.8) | copy-start | bytes 7077892
  18.4 1.2 %copy-start.1 = (bf16[2,16,128,128]{3,2,1,0:T(8,128)(2,1)S(1)}, bf16[2,16,128,128]{3,2,1,0:T(8,128)(2,1)}, u32[]{:S(2)}) copy-start(bf16[2,16,128,128]{3,2,1,0:T(8,128)(2,1)} %get-tuple-element.7.patches) | copy-start | bytes 3145732
  19.6 0.7 %copy-start.3 = (s32[2,2,128]{2,1,0:T(2,128)S(1)}, s32[2,2,128]{2,1,0:T(2,128)}, u32[]{:S(2)}) copy-start(s32[2,2,128]{2,1,0:T(2,128)} %get-tuple-element.6.cands.cand_rows) | copy-start | bytes 6148
  23.7 0.6 %copy-start.2 = (f32[2,8,384]{2,1,0:T(8,128)}, f32[2,8,384]{2,1,0:T(8,128)S(1)}, u32[]{:S(2)}) copy-start(f32[2,8,384]{2,1,0:T(8,128)S(1)} %match.1.scored) | copy-start | bytes 73732

commit v4 on v3

--- a/solution.py
+++ b/solution.py
@@ -84,7 +84,12 @@
         in_specs=[anywhere, anywhere],
         out_specs=(anywhere, anywhere),
         scratch_shapes=[dma((2, 2)), dma((2, 2))],
-        compiler_params=pltpu.CompilerParams(collective_id=1, has_side_effects=True),
+        compiler_params=pltpu.CompilerParams(
+            collective_id=1, has_side_effects=True, vmem_limit_bytes=4 * 1024 * 1024
+        ),
+        cost_estimate=pl.CostEstimate(
+            flops=0, bytes_accessed=32 * patches.size * patches.dtype.itemsize, transcendentals=0
+        ),
         name="hand_over",
     )(patches, cands)
 
@@ -207,7 +212,7 @@
             pltpu.VMEM((patch_size, patch_size), jnp.float32),
             pltpu.VMEM((5, P_SIZE * NS * 8, 128), jnp.float32),
         ],
-        compiler_params=pltpu.CompilerParams(vmem_limit_bytes=40 * 1024 * 1024),
+        compiler_params=pltpu.CompilerParams(vmem_limit_bytes=24 * 1024 * 1024),
         name="match",
     )(live, cands, cands, patches, frames)
 

time: 57.9 us -> 56.7 us (0.979)
  Pallas kernels: 48.6 us -> 47.1 us
    pallas_call x1, Pallas kernels: 29.9 us -> 28.7 us  [mesh_call(): pl.pallas_call(functools.partial(mesh_kernel, (rows, cols)), out_shape=(j...]
where the time goes in v4:
time: 56.7 us; the launch traced here: 56.3 us
  Pallas kernels  47.1 us (83%)
  local copies, waits for them, and re-layouts  7.52 us (13%)
  matrix products  0.99 us (2%)
  between operations  0.7 us (1%)
    pallas_call x1, Pallas kernels, mesh_call(): pl.pallas_call(functools.partial(mesh_kernel, (rows, cols)), out_shape=(j...  28.7 us
    pallas_call x1, Pallas kernels, pass_call(): pl.pallas_call(functools.partial(pass_kernel, (lax.axis_size('row'), lax....  14.9 us
    unnamed x16, local copies, waits for them, and re-layouts  6.26 us
    pallas_call x1, Pallas kernels, match_call(): pl.pallas_call(match_kernel, out_shape=jax.ShapeDtypeStruct((2, 8, CELLS...  3.45 us
    pallas_call x1, local copies, waits for them, and re-layouts, mesh_call(): pl.pallas_call(functools.partial(mesh_kernel, (rows, cols)), out_shape=(j...  1.26 us

profile of v4, /device:TPU:0, one launch (start us, length us, event | category | flops | bytes accessed | tf_op | source)
XLA Modules:
  0.0 56.3 jit_solution(2320153331061833517)
XLA Ops:
  0.6 0.0 copy-start.6
  0.6 0.0 copy-start.5
  0.7 0.0 copy-start.1
  0.7 1.2 %copy-done.1 = bf16[1,1,2,16,128,128]{5,4,3,2,1,0:T(8,128)(2,1)S(1)} copy-done((bf16[1,1,2,16,128,128]{5,4,3,2,1,0:T(8,128)(2,1)S(1)}, bf16[1,1,2,16,128,128]{5,4,3,2,1,0:T(8,128)(2,1)}, u32[]{:S(2)}) %copy-start.1) | copy-done | bytes 1048600
  1.9 0.0 copy-start.3
  1.9 0.7 %copy-done.3 = s32[1,1,2,2,128]{4,3,2,1,0:T(2,128)S(1)} copy-done((s32[1,1,2,2,128]{4,3,2,1,0:T(2,128)S(1)}, s32[1,1,2,2,128]{4,3,2,1,0:T(2,128)}, u32[]{:S(2)}) %copy-start.3) | copy-done | bytes 2072
  2.6 0.0 copy-start.4
  2.6 14.9 %hand_over.1 = (bf16[2,16,128,128]{3,2,1,0:T(8,128)(2,1)S(1)}, s32[2,2,128]{2,1,0:T(2,128)S(1)}) custom-call(bf16[2,16,128,128]{3,2,1,0:T(8,128)(2,1)S(1)} %bitcast.8, s32[2,2,128]{2,1,0:T(2,128)S(1)} %bitcast.9), custom_call_target="tpu_custom_call" | custom-call | bytes 33554432 | tf_op jit(solution)/shard_map/hand_over/pallas_call | solution.py:78
  17.5 0.8 %copy.9.live = s32[8,4,2]{2,1,0:T(4,128)S(1)} copy(s32[8,4,2]{0,2,1:T(2,128)} %param.10) | data formatting | bytes 512 | tf_op args[3]
  18.3 0.0 copy-start
  18.3 1.7 %copy-done = bf16[1,1,2,16,36864]{4,3,2,1,0:T(8,128)(2,1)S(1)} copy-done((bf16[1,1,2,16,36864]{4,3,2,1,0:T(8,128)(2,1)S(1)}, bf16[1,1,2,16,36864]{4,3,2,1,0:T(8,128)(2,1)}, u32[]{:S(2)}) %copy-start) | copy-done | bytes 2359320
  19.9 3.5 %match.1.scored = f32[2,8,384]{2,1,0:T(8,128)S(1)} custom-call(s32[8,4,2]{2,1,0:T(4,128)S(1)} %copy.9.live, s32[2,2,128]{2,1,0:T(2,128)S(1)} %get-tuple-element.6.cands.cand_rows, s32[2,2,128]{2,1,0:T(2,128)S(1)} %get-tuple-element.6.cands.cand_rows, bf16[2,16,128,128]{3,2,1,0:T(8,128)(2,1)S(1)} %get-tuple-element.7.patches, bf16[2,16,36864]{2,1,0:T(8,128)(2,1)S(1)} %bitcast.7), custom_call_target="tpu_custom_call" | custom-call | tf_op jit(solution)/shard_map/match/pallas_call | solution.py:205
  23.4 0.0 copy-start.2
  23.4 0.6 %copy-done.2 = f32[2,8,384]{2,1,0:T(8,128)} copy-done((f32[2,8,384]{2,1,0:T(8,128)}, f32[2,8,384]{2,1,0:T(8,128)S(1)}, u32[]{:S(2)}) %copy-start.2) | copy-done | bytes 24600
  24.0 0.0 copy-done.4
  24.0 0.0 copy-done.5
  24.1 0.0 copy-done.6
  24.1 1.0 %fusion.springs = f32[8,256]{1,0:T(8,128)} fusion(s32[705]{0:T(1024)S(1)} %get-tuple-element.11, f32[705]{0:T(1024)S(1)} %reduce.1, s32[705]{0:T(1024)S(1)} %get-tuple-element.10, s32[8]{0:T(128)S(1)} %copy-done.6), kind=kOutput, calls=%fused_computation.1 | convolution fusion | flops 17517840 | bytes 16684 | tf_op jit(solution)/shard_map/dot_general | solution.py:430
  25.1 28.7 %mesh.1 = (f32[2,3,16]{2,1,0:T(4,128)}, f32[2,256]{1,0:T(2,128)}) custom-call(f32[2,8,384]{2,1,0:T(8,128)} %copy-done.2, f32[8,256]{1,0:T(8,128)} %fusion.springs), custom_call_target="tpu_custom_call" | custom-call | tf_op jit(solution)/shard_map/mesh/pallas_call | solution.py:393
  53.8 1.3 %copy.12 = f32[2,3,16]{2,0,1:T(2,128)} copy(f32[2,3,16]{2,1,0:T(4,128)} %get-tuple-element.8) | data formatting | bytes 768 | tf_op jit(solution)/shard_map/mesh/pallas_call | solution.py:393
  55.1 1.3 %copy.14 = f32[1,1,2,256]{3,2,1,0:T(2,128)} copy(f32[1,1,2,256]{3,2,1,0:T(2,128)} %bitcast.11) | data formatting | bytes 4096
  (2 shorter events, 0.0 us)
Async XLA Ops:
  0.6 23.4 %copy-start.6 = (s32[8]{0:T(128)S(1)}, s32[8]{0:T(128)}, u32[]{:S(2)}) copy-start(s32[8]{0:T(128)} %constant.4.clone) | copy-start | bytes 100
  0.6 23.4 %copy-start.5 = (f32[1,705]{1,0:T(1,128)S(1)}, f32[1,705]{1,0:T(1,128)}, u32[]{:S(2)}) copy-start(f32[1,705]{1,0:T(1,128)} %param.12) | copy-start | bytes 8464
  0.7 1.2 %copy-start.1 = (bf16[1,1,2,16,128,128]{5,4,3,2,1,0:T(8,128)(2,1)S(1)}, bf16[1,1,2,16,128,128]{5,4,3,2,1,0:T(8,128)(2,1)}, u32[]{:S(2)}) copy-start(bf16[1,1,2,16,128,128]{5,4,3,2,1,0:T(8,128)(2,1)} %param.7) | copy-start | bytes 3145732
  1.9 0.7 %copy-start.3 = (s32[1,1,2,2,128]{4,3,2,1,0:T(2,128)S(1)}, s32[1,1,2,2,128]{4,3,2,1,0:T(2,128)}, u32[]{:S(2)}) copy-start(s32[1,1,2,2,128]{4,3,2,1,0:T(2,128)} %param.9) | copy-start | bytes 6148
  2.6 21.4 %copy-start.4 = (s32[1,2,705]{2,1,0:T(2,128)S(1)}, s32[1,2,705]{2,1,0:T(2,128)}, u32[]{:S(2)}) copy-start(s32[1,2,705]{2,1,0:T(2,128)} %param.11) | copy-start | bytes 16924
  18.3 1.7 %copy-start = (bf16[1,1,2,16,36864]{4,3,2,1,0:T(8,128)(2,1)S(1)}, bf16[1,1,2,16,36864]{4,3,2,1,0:T(8,128)(2,1)}, u32[]{:S(2)}) copy-start(bf16[1,1,2,16,36864]{4,3,2,1,0:T(8,128)(2,1)} %param.8) | copy-start | bytes 7077892
  23.4 0.6 %copy-start.2 = (f32[2,8,384]{2,1,0:T(8,128)}, f32[2,8,384]{2,1,0:T(8,128)S(1)}, u32[]{:S(2)}) copy-start(f32[2,8,384]{2,1,0:T(8,128)S(1)} %match.1.scored) | copy-start | bytes 73732
